TPU v7x, 256 devices: a whole 4x4x8 slice. The times are simulated.
256 devices in a mesh: dp: 32 (over z_lo, x, core), mp: 8 (over z_hi, y).
Axes of the slice: x: 4, y: 4, z: 8 (z_hi: 2, z_lo: 4; z = z_hi * 4 + z_lo), core: 2. Of those that a mesh axis runs over, the one named last changes fastest.
Arguments:
- clean: bfloat16 [32, 1024, 1280], P('dp', 'mp'), may hold values from -6 to 6
- noise: bfloat16 [32, 1024, 1280], P('dp', 'mp'), may hold values from -6 to 6
- tsteps: int32 [32], P('dp'), may hold values from 0 to 999
- alpha_tab: float32 [1000], replicated, may hold values from 0.3 to 0.99
- weight_tab: float32 [1000], replicated, may hold values from 0.1 to 3
- norm1_gain: float32 [1280], replicated, may hold values from 0.1 to 1.9
- norm2_gain: float32 [1280], replicated, may hold values from 0.1 to 1.9
- wqkv: bfloat16 [3, 1280, 1280], P(None, 'dp', 'mp'), may hold values from -4 to 4
- wout: bfloat16 [1280, 1280], P('dp', 'mp'), may hold values from -0.625 to 0.625
- wgate: bfloat16 [1280, 5120], P('dp', 'mp'), may hold values from -0.15625 to 0.15625
- wvalue: bfloat16 [1280, 5120], P('dp', 'mp'), may hold values from -0.15625 to 0.15625
- wdown: bfloat16 [5120, 1280], P('mp', 'dp'), may hold values from -0.078125 to 0.078125
Outputs:
- denoised: float32 [32, 1024, 1280], P('dp', 'mp')
- loss: float32 [], replicated
All inputs are finite; a program needn't handle non-finite values.
Results may differ from a plain program's by a relative error of at most 0.02.
Values may be sent and summed in bfloat16 or wider, within the bound.
A program may use at most 64 MiB of HBM per device.

v0:
```python
import jax
import jax.numpy as jnp
from jax import lax
from jax.sharding import Mesh
from jax.sharding import PartitionSpec as P

D = 1280
HEADS = 20
HEAD = 64
L = 1024
MP = ("mp_0", "mp_1")
DP = ("dp_0", "dp_1", "dp_2")
DP_MP = ("dp_0", "dp_1", "dp_2", "mp_0", "mp_1")


def copy_for_each(value, axis):
    length = lax.axis_size(axis)
    return lax.all_to_all(
        jnp.broadcast_to(value[None], (length, *value.shape)), axis, 0, 0, tiled=True
    )


def in_order(blocks, dim):
    blocks = jnp.moveaxis(blocks, 0, dim)
    dims = blocks.shape
    return blocks.reshape(*dims[:dim], dims[dim] * dims[dim + 1], *dims[dim + 2 :])


def gathered_copies(value, axis, dim):
    blocks = copy_for_each(value, axis)
    return in_order(blocks, dim)


def sent_together(arrays, axis, dim, along):
    ends, at = ([], 0)
    for a in arrays[:-1]:
        at += a.shape[along]
        ends.append(at)
    both = jnp.concatenate(arrays, axis=along)
    return tuple(jnp.split(lax.all_gather(both, axis, axis=dim, tiled=True), ends, axis=along))


def whole_of(value, axes, dim):
    far, near = axes
    blocks = copy_for_each(copy_for_each(value, far), near)
    return in_order(blocks.swapaxes(0, 1).reshape(-1, *value.shape), dim)


def sum_in_order(blocks, axes, order):
    inside = blocks.shape[1:]
    blocks = blocks.reshape(*(lax.axis_size(a) for a in axes), *inside)
    blocks = jnp.moveaxis(blocks, order, range(len(axes))).reshape(-1, *inside)
    for k in order:
        blocks = lax.psum_scatter(blocks, axes[k], scatter_dimension=0, tiled=True)
    return blocks[0]


def in_blocks(value, dim, length):
    before, after = (value.shape[:dim], value.shape[dim + 1 :])
    return jnp.moveaxis(value.reshape(*before, length, -1, *after), dim, 0)


def sum_by_axis(value, axes, order, dim):
    length = lax.axis_size(axes)
    return sum_in_order(in_blocks(value, dim, length), axes, order)


def by_axis(value, axes):
    for axis in axes:
        value = lax.psum(value, axis)
    return value


def lookup(steps, table):
    match = steps[:, None] == jnp.arange(table.shape[0], dtype=jnp.int32)[None, :]
    return jnp.sum(jnp.where(match, table[None, :], jnp.zeros((), table.dtype)), axis=1)


def layer_norm(values, gain):
    wide = values.astype(jnp.float32)
    center = wide - jnp.mean(wide, axis=-1, keepdims=True)
    spread = jnp.mean(center * center, axis=-1, keepdims=True)
    return (center * lax.rsqrt(spread + 1e-05) * gain).astype(jnp.bfloat16)


def make_adder(flat, piece):
    return jnp.einsum("rn,tnc->trc", flat, piece, preferred_element_type=jnp.float32)


def attend(operands):
    query_one, keys_one, values_one = operands
    rows = query_one.shape[0]
    total = keys_one.shape[0]
    scores = jnp.einsum(
        "qhd,khd->hqk",
        query_one.reshape(rows, HEADS, HEAD),
        keys_one.reshape(total, HEADS, HEAD),
        preferred_element_type=jnp.float32,
    ) * HEAD ** (-0.5)
    probs = jax.nn.softmax(scores, axis=-1).astype(jnp.bfloat16)
    mixed = jnp.einsum(
        "hqk,khd->qhd",
        probs,
        values_one.reshape(total, HEADS, HEAD),
        preferred_element_type=jnp.float32,
    )
    return mixed.astype(jnp.bfloat16).reshape(rows, D)


def shards(
    clean,
    noise,
    tsteps,
    alpha_tab,
    weight_tab,
    norm1_gain,
    norm2_gain,
    wqkv,
    wout,
    wgate,
    wvalue,
    wdown,
):
    samples, local_rows, width = clean.shape
    alpha = lookup(tsteps, alpha_tab)
    sigma = jnp.sqrt(1.0 - alpha * alpha)
    weight = lookup(tsteps, weight_tab)
    noised = (
        alpha[:, None, None] * clean.astype(jnp.float32)
        + sigma[:, None, None] * noise.astype(jnp.float32)
    ).astype(jnp.bfloat16)
    normed1 = layer_norm(noised, norm1_gain)
    full_cols = gathered_copies(wqkv, MP, 2)
    flat = normed1.reshape(samples * local_rows, width)
    projected = make_adder(flat, lax.all_gather(full_cols, DP, axis=1, tiled=True)).astype(
        jnp.bfloat16
    )
    query = projected[0].reshape(samples, local_rows, width)
    keys_part = projected[1].reshape(samples, local_rows, width)
    values_part = projected[2].reshape(samples, local_rows, width)
    keys_all, values_all = sent_together((keys_part, values_part), MP, 1, 0)
    mixed = lax.map(attend, (query, keys_all, values_all))
    mixed_flat = mixed.reshape(samples * local_rows, width)
    out_cols = gathered_copies(wout, MP, 1)
    part = mixed_flat
    projected_out = jnp.dot(
        part, whole_of(out_cols, (("dp_0", "dp_1"), "dp_2"), 0), preferred_element_type=jnp.float32
    )
    resid = (noised.astype(jnp.float32) + projected_out.reshape(samples, local_rows, width)).astype(
        jnp.bfloat16
    )
    normed2 = layer_norm(resid, norm2_gain)
    ff_in = lax.all_gather(normed2, MP, axis=1, tiled=True)
    all_rows = ff_in.shape[1]
    ff_flat = ff_in.reshape(samples * all_rows, width)
    pieces = sent_together((wgate, wvalue), DP, 0, 1)
    part = ff_flat
    gate = jnp.dot(part, pieces[0], preferred_element_type=jnp.float32)
    value = jnp.dot(part, pieces[1], preferred_element_type=jnp.float32)
    hidden = (jax.nn.gelu(gate, approximate=False) * value).astype(jnp.bfloat16)
    block_sum = jnp.dot(
        hidden, whole_of(wdown, (("dp_0", "dp_1"), "dp_2"), 1), preferred_element_type=jnp.float32
    )
    ff_out = sum_by_axis(
        block_sum.reshape(samples, all_rows, width).astype(jnp.bfloat16), MP, (1, 0), 1
    ).astype(jnp.float32)
    prediction = resid.astype(jnp.float32) + ff_out
    denoised = (noised.astype(jnp.float32) - sigma[:, None, None] * prediction) / alpha[
        :, None, None
    ]
    error = denoised - clean.astype(jnp.float32)
    local_terms = jnp.sum(weight * jnp.sum(error * error, axis=(1, 2))) / (L * D)
    loss = by_axis(local_terms, DP_MP)
    return (denoised, loss)


def solution(mesh):
    split = Mesh(mesh.devices.reshape(4, 4, 2, 2, 4), ("dp_0", "dp_1", "dp_2", "mp_0", "mp_1"))
    in_specs = (
        P(DP, MP, None),
        P(DP, MP, None),
        P(DP),
        P(),
        P(),
        P(),
        P(),
        P(None, DP, MP),
        P(DP, MP),
        P(DP, MP),
        P(DP, MP),
        P(MP, DP),
    )
    out_specs = (P(DP, MP, None), P())
    return jax.shard_map(
        shards, mesh=split, in_specs=in_specs, out_specs=out_specs, check_vma=False
    )
```

profile of v0, /device:TPU:1, one launch (start us, length us, event | category | flops | bytes accessed | tf_op | source)
XLA Modules:
  0.0 534.2 jit_solution(18051994592071202623)
XLA Ops:
  7.3 0.9 broadcast_in_dim.27
  8.2 23.8 %all_to_all.30 = bf16[8,3,40,160]{3,2,1,0:T(8,128)(2,1)S(1)} all-to-all(bf16[8,3,40,160]{3,2,1,0:T(8,128)(2,1)S(1)} %broadcast_in_dim.27), channel_id=1, replica_groups=mesh['dp_0'=4,'dp_1'=4,'dp_2'=2,'mp_0'=2,'mp_1'=4] {'mp_0','mp_1'}, dimensions={0} | all-to-all | bytes 614400 | tf_op jit(solution)/shard_map/all_to_all | solution.py:18
  32.0 0.1 copy.23
  32.1 1.2 reshape.152
  33.3 0.0 all-gather.7.cloned.1.call-start
  34.0 0.6 select_reduce_fusion.1
  35.8 0.8 convert_reduce_fusion
  36.6 0.2 fusion.41
  36.9 69.3 %all-gather.5.cloned.1.call-done = bf16[3,1280,1280]{2,1,0:T(8,128)(2,1)} async-done(((bf16[3,40,1280]{2,1,0:T(8,128)(2,1)}), bf16[3,1280,1280]{2,1,0:T(8,128)(2,1)}) %all-gather.5.cloned.1.call-update) | async-done | bytes 9830416 | tf_op jit(solution)/shard_map/all_gather | solution.py:135
  106.2 5.3 fusion.21
  111.5 0.9 concatenate.8
  112.4 17.0 %all_to_all.31 = bf16[8,40,160]{2,1,0:T(8,128)(2,1)S(1)} all-to-all(bf16[8,40,160]{2,1,0:T(8,128)(2,1)S(1)} %broadcast_in_dim.28), channel_id=1, replica_groups=mesh['dp_0'=4,'dp_1'=4,'dp_2'=2,'mp_0'=2,'mp_1'=4] {'mp_0','mp_1'}, dimensions={0} | all-to-all | bytes 204800 | tf_op jit(solution)/shard_map/all_to_all | solution.py:18
  129.5 0.2 broadcast_in_dim.29
  129.7 1.3 broadcast_in_dim.30
  131.0 4.3 all-to-all-start.2
  135.4 0.6 pad_maximum_fusion
  136.1 0.0 all-gather.9.cloned.1.call-start
  136.1 94.0 %all-to-all-done.2 = bf16[16,40,1280]{2,1,0:T(8,128)(2,1)S(1)} async-done(((bf16[16,40,1280]{2,1,0:T(8,128)(2,1)}), bf16[16,40,1280]{2,1,0:T(8,128)(2,1)S(1)}, u32[]{:S(2)}, u32[]{:S(2)}) %all-to-all-start.2) | async-done | bytes 1638432 | tf_op jit(solution)/shard_map/all_to_all | solution.py:18
  230.1 0.2 broadcast_in_dim.31
  230.3 6.6 %all_to_all.32 = bf16[2,16,40,1280]{3,2,1,0:T(8,128)(2,1)S(1)} all-to-all(bf16[2,16,40,1280]{3,2,1,0:T(8,128)(2,1)S(1)} %broadcast_in_dim.31), channel_id=1, replica_groups=mesh['dp_0'=4,'dp_1'=4,'dp_2'=2,'mp_0'=2,'mp_1'=4] {'dp_2'}, dimensions={0} | all-to-all | bytes 6553600 | tf_op jit(solution)/shard_map/all_to_all | solution.py:18
  236.9 1.9 copy.28
  238.8 0.9 copy.25
  239.7 4.4 fusion.88
  244.1 4.5 copy.24
  248.6 2.7 copy.26
  251.3 9.3 %fusion.89 = (f32[20,128]{1,0:T(8,128)S(1)}, f32[20,128,1024]{2,1,0:T(8,128)}) fusion(bf16[128,20,64]{0,2,1:T(8,128)(2,1)} %bitcast.72, bf16[1024,20,64]{0,2,1:T(8,128)(2,1)} %bitcast.66), kind=kOutput, calls=%fused_computation.105 | convolution fusion | flops 343409664 | bytes 13445120 | tf_op jit(solution)/shard_map/while/body/eval_jaxpr/sub | solution.py:100
  260.6 6.2 %fusion.28 = bf16[20,64,128]{2,1,0:T(8,128)(2,1)S(1)} fusion(bf16[1024,20,64]{0,2,1:T(8,128)(2,1)S(1)} %bitcast.65, f32[20,128,1024]{2,1,0:T(8,128)} %get-tuple-element.24, f32[20,128]{1,0:T(8,128)S(1)} %get-tuple-element.23), kind=kOutput, calls=%fused_computation.40 | convolution fusion | flops 340951040 | bytes 13445120 | tf_op jit(solution)/shard_map/while/body/eval_jaxpr/hqk,khd->qhd/dot_general | solution.py:101
  266.8 0.7 fusion.90
  267.5 0.2 multiply_reduce_fusion.1
  267.8 0.9 multiply_convert_fusion
  268.7 0.1 broadcast_in_dim.32
  268.8 33.2 %all_to_all.33 = bf16[16,640,40]{1,2,0:T(8,128)(2,1)S(1)} all-to-all(bf16[16,640,40]{1,2,0:T(8,128)(2,1)S(1)} %broadcast_in_dim.32), channel_id=1, replica_groups=mesh['dp_0'=4,'dp_1'=4,'dp_2'=2,'mp_0'=2,'mp_1'=4] {'dp_0','dp_1'}, dimensions={0} | all-to-all | bytes 1638400 | tf_op jit(solution)/shard_map/all_to_all | solution.py:18
  302.0 0.1 broadcast_in_dim.33
  302.1 6.3 %all_to_all.34 = bf16[2,16,640,40]{2,3,1,0:T(8,128)(2,1)S(1)} all-to-all(bf16[2,16,640,40]{2,3,1,0:T(8,128)(2,1)S(1)} %broadcast_in_dim.33), channel_id=1, replica_groups=mesh['dp_0'=4,'dp_1'=4,'dp_2'=2,'mp_0'=2,'mp_1'=4] {'dp_2'}, dimensions={0} | all-to-all | bytes 3276800 | tf_op jit(solution)/shard_map/all_to_all | solution.py:18
  308.4 0.1 copy.29
  308.6 82.6 %all-gather.9.cloned.1.call-done = bf16[1,1024,1280]{2,1,0:T(8,128)(2,1)} async-done(((bf16[1,128,1280]{2,1,0:T(8,128)(2,1)}), bf16[1,1024,1280]{2,1,0:T(8,128)(2,1)}) %all-gather.9.cloned.1.call-update) | async-done | bytes 2621456 | tf_op jit(solution)/shard_map/all_gather | solution.py:153
  391.2 5.9 %fusion.10 = f32[1024,640]{1,0:T(8,128)} fusion(bf16[1,1024,1280]{2,1,0:T(8,128)(2,1)} %all-gather.9.cloned.1.call-done, bf16[1280,1280]{1,0:T(8,128)(2,1)} %all-gather.11.cloned.1.call-done), kind=kOutput, calls=%fused_computation.14 | convolution fusion | flops 1677721600 | bytes 6881280 | tf_op jit(solution)/shard_map/dot_general | solution.py:159
  397.1 12.9 %convolution_convert_fusion = bf16[1024,1280]{1,0:T(8,128)(2,1)} fusion(bf16[640,1280]{0,1:T(8,128)(2,1)S(1)} %bitcast.69, f32[1024,640]{1,0:T(8,128)} %fusion.10, bf16[1,1024,1280]{2,1,0:T(8,128)(2,1)} %all-gather.9.cloned.1.call-done, bf16[1280,1280]{1,0:T(8,128)(2,1)} %all-gather.11.cloned.1.call-done), kind=kOutput, calls=%fused_computation.8 | convolution fusion | flops 3400007680 | bytes 11141120 | tf_op jit(solution)/shard_map/dot_general | solution.py:161
  410.0 3.4 copy.30
  413.5 33.4 %reduce-scatter.3.cloned.1.call-done = bf16[2,1,128,1280]{3,2,1,0:T(8,128)(2,1)} async-done(((bf16[8,1,128,1280]{3,2,1,0:T(8,128)(2,1)}), bf16[2,1,128,1280]{3,2,1,0:T(8,128)(2,1)}) %reduce-scatter.3.cloned.1.call-update) | async-done | bytes 655376 | tf_op jit(solution)/shard_map/reduce_scatter | solution.py:54
  446.9 0.7 select_reduce_fusion
  447.6 33.8 %reduce-scatter.5.cloned.1.call-done = bf16[1,1,128,1280]{3,2,1,0:T(8,128)(2,1)} async-done(((bf16[2,1,128,1280]{3,2,1,0:T(8,128)(2,1)}), bf16[1,1,128,1280]{3,2,1,0:T(8,128)(2,1)}) %reduce-scatter.5.cloned.1.call-update) | async-done | bytes 327696 | tf_op jit(solution)/shard_map/reduce_scatter | solution.py:54
  481.4 3.2 fusion.47
  485.9 7.3 %psum.35 = f32[]{:T(128)} all-reduce(f32[]{:T(128)S(6)} %div.40), channel_id=1, replica_groups=mesh['dp_0'=4,'dp_1'=4,'dp_2'=2,'mp_0'=2,'mp_1'=4] {'dp_0'}, use_global_device_ids=true, to_apply=%region_11.12 | all-reduce | flops 1 | bytes 8 | tf_op jit(solution)/shard_map/psum | solution.py:70
  493.2 9.0 %psum.36 = f32[]{:T(128)} all-reduce(f32[]{:T(128)} %psum.35), channel_id=1, replica_groups=mesh['dp_0'=4,'dp_1'=4,'dp_2'=2,'mp_0'=2,'mp_1'=4] {'dp_1'}, use_global_device_ids=true, to_apply=%region_12.13 | all-reduce | flops 1 | bytes 8 | tf_op jit(solution)/shard_map/psum | solution.py:70
  502.2 7.8 %psum.37 = f32[]{:T(128)} all-reduce(f32[]{:T(128)} %psum.36), channel_id=1, replica_groups=mesh['dp_0'=4,'dp_1'=4,'dp_2'=2,'mp_0'=2,'mp_1'=4] {'dp_2'}, use_global_device_ids=true, to_apply=%region_13.14 | all-reduce | flops 1 | bytes 8 | tf_op jit(solution)/shard_map/psum | solution.py:70
  510.0 8.3 %psum.38 = f32[]{:T(128)} all-reduce(f32[]{:T(128)} %psum.37), channel_id=1, replica_groups=mesh['dp_0'=4,'dp_1'=4,'dp_2'=2,'mp_0'=2,'mp_1'=4] {'mp_0'}, use_global_device_ids=true, to_apply=%region_14.15 | all-reduce | flops 1 | bytes 8 | tf_op jit(solution)/shard_map/psum | solution.py:70
  518.3 9.0 %psum.39 = f32[]{:T(128)} all-reduce(f32[]{:T(128)} %psum.38), channel_id=1, replica_groups=mesh['dp_0'=4,'dp_1'=4,'dp_2'=2,'mp_0'=2,'mp_1'=4] {'mp_1'}, use_global_device_ids=true, to_apply=%region_15.16 | all-reduce | flops 1 | bytes 8 | tf_op jit(solution)/shard_map/psum | solution.py:70
  (43 shorter events, 0.4 us)
Async XLA Ops:
  7.2 26.8 %copy-start.10 = (f32[1000]{0:T(1024)S(1)}, f32[1000]{0:T(1024)}, u32[]{:S(2)}) copy-start(f32[1000]{0:T(1024)} %param.15) | copy-start | bytes 12004
  7.2 28.6 %copy-start.2 = (bf16[1,128,1280]{2,1,0:T(8,128)(2,1)S(1)}, bf16[1,128,1280]{2,1,0:T(8,128)(2,1)}, u32[]{:S(2)}) copy-start(bf16[1,128,1280]{2,1,0:T(8,128)(2,1)} %param.12) | copy-start | bytes 983044
  7.2 28.6 %copy-start.3 = (bf16[1,128,1280]{2,1,0:T(8,128)(2,1)S(1)}, bf16[1,128,1280]{2,1,0:T(8,128)(2,1)}, u32[]{:S(2)}) copy-start(bf16[1,128,1280]{2,1,0:T(8,128)(2,1)} %param.13) | copy-start | bytes 983044
  7.2 99.0 %copy-start.8 = (f32[1280]{0:T(1024)S(1)}, f32[1280]{0:T(1024)}, u32[]{:S(2)}) copy-start(f32[1280]{0:T(1024)} %param.17) | copy-start | bytes 15364
  7.2 99.0 %all-gather.5.cloned.1.call-start = ((), (), s32[]{:S(2)}) async-start(), calls=%async_computation.8 | async-start | bytes 10137600 | tf_op jit(solution)/shard_map/all_gather | solution.py:135
  33.3 206.4 %all-gather.7.cloned.1.call-start = ((), (), s32[]{:S(2)}) async-start(), calls=%async_computation.9 | async-start | bytes 5898240 | tf_op jit(solution)/shard_map/all_gather | solution.py:40
  36.9 75.5 %copy-start.7 = (bf16[40,160]{1,0:T(8,128)(2,1)S(1)}, bf16[40,160]{1,0:T(8,128)(2,1)}, u32[]{:S(2)}) copy-start(bf16[40,160]{1,0:T(8,128)(2,1)} %param.20) | copy-start | bytes 38404
  129.4 5.9 %copy-start.4 = (bf16[40,640]{1,0:T(8,128)(2,1)S(1)}, bf16[40,640]{1,0:T(8,128)(2,1)}, u32[]{:S(2)}) copy-start(bf16[40,640]{1,0:T(8,128)(2,1)} %param.22) | copy-start | bytes 153604
  129.5 5.9 %copy-start.5 = (bf16[40,640]{1,0:T(8,128)(2,1)S(1)}, bf16[40,640]{1,0:T(8,128)(2,1)}, u32[]{:S(2)}) copy-start(bf16[40,640]{1,0:T(8,128)(2,1)} %param.21) | copy-start | bytes 153604
  131.0 99.1 %all-to-all-start.2 = ((bf16[16,40,1280]{2,1,0:T(8,128)(2,1)}), bf16[16,40,1280]{2,1,0:T(8,128)(2,1)S(1)}, u32[]{:S(2)}, u32[]{:S(2)}) async-start(bf16[16,40,1280]{2,1,0:T(8,128)(2,1)} %broadcast_in_dim.30), calls=%async_computation.2 | async-start | bytes 3276800 | tf_op jit(solution)/shard_map/all_to_all | solution.py:18
  135.3 173.3 %all-gather.11.cloned.1.call-start = ((), (), s32[]{:S(2)}) async-start(), calls=%async_computation.11 | async-start | bytes 3379200 | tf_op jit(solution)/shard_map/all_gather | solution.py:40
  136.1 255.1 %all-gather.9.cloned.1.call-start = ((), (), s32[]{:S(2)}) async-start(), calls=%async_computation.10 | async-start | bytes 2949120 | tf_op jit(solution)/shard_map/all_gather | solution.py:153
  251.3 9.3 %copy-start.1 = (bf16[1,1024,1280]{1,2,0:T(8,128)(2,1)S(1)}, bf16[1,1024,1280]{1,2,0:T(8,128)(2,1)}, u32[]{:S(2)}) copy-start(bf16[1,1024,1280]{1,2,0:T(8,128)(2,1)} %copy.24) | copy-start | bytes 7864324
  260.6 6.2 %copy-start = (bf16[2,16,40,1280]{3,2,0,1:T(8,128)(2,1)S(1)}, bf16[2,16,40,1280]{3,2,0,1:T(8,128)(2,1)}, u32[]{:S(2)}) copy-start(bf16[2,16,40,1280]{3,2,0,1:T(8,128)(2,1)} %copy.28) | copy-start | bytes 9830404
  266.8 1.0 copy-start.9
  266.8 1.9 copy-start.6
  268.7 178.2 %reduce-scatter.3.cloned.1.call-start = ((), (), s32[]{:S(2)}) async-start(), calls=%async_computation.12 | async-start | bytes 3276800 | tf_op jit(solution)/shard_map/reduce_scatter | solution.py:54
  413.5 33.5 %copy-start.11 = (f32[1000]{0:T(1024)S(1)}, f32[1000]{0:T(1024)}, u32[]{:S(2)}) copy-start(f32[1000]{0:T(1024)} %param.16) | copy-start | bytes 12004
  413.5 67.9 %reduce-scatter.5.cloned.1.call-start = ((), (), s32[]{:S(2)}) async-start(), calls=%async_computation.13 | async-start | bytes 983040 | tf_op jit(solution)/shard_map/reduce_scatter | solution.py:54
Sparse Core Ops, SparseCore 0:
  33.4 72.6 all-gather.4
  112.5 99.7 all-gather.6
  214.1 91.9 all-gather.10
  309.2 81.9 all-gather.8
  413.6 33.2 reduce-scatter.2
  449.3 32.0 reduce-scatter.4
where the time goes:
time: 536 us; the launch traced here: 534 us
  waiting for transfers between devices  313 us (58%)
  blocking collectives  128 us (24%)
  matrix products  40.3 us (8%)
  local copies, waits for them, and re-layouts  23.1 us (4%)
  between operations  17.5 us (3%)
  other arithmetic  7.28 us (1%)
    all_to_all x1, waiting for transfers between devices, copy_for_each(): lax.all_to_all(jnp.broadcast_to(value[None], (length, *value.shape)), axi...  94 us
    all_to_all x5, blocking collectives, copy_for_each(): lax.all_to_all(jnp.broadcast_to(value[None], (length, *value.shape)), axi...  86.8 us
    all_gather x1, waiting for transfers between devices, shards(): ff_in = lax.all_gather(normed2, MP, axis=1, tiled=True)  82.6 us
    all_gather x1, waiting for transfers between devices, shards(): lax.all_gather(full_cols, DP, axis=1, tiled=True)  69.3 us
    reduce_scatter x2, waiting for transfers between devices, sum_in_order(): blocks = lax.psum_scatter(blocks, axes[k], scatter_dimension=0, tiled=True)  67.1 us
    psum x5, blocking collectives, by_axis(): value = lax.psum(value, axis)  41.4 us
    dot_general x1, matrix products, shards(): jnp.dot(hidden, whole_of(wdown, (('dp_0', 'dp_1'), 'dp_2'), 1), preferred...  12.9 us
    split x3, local copies, waits for them, and re-layouts, sent_together(): jnp.split(lax.all_gather(both, axis, axis=dim, tiled=True), ends, axis=al...  11.6 us
  transfers between devices with their start and end apart: 7, of which 5 were waited for; matrix products, arithmetic and copies ran while one was open for 7% of the time, Pallas kernels for 0%

commit v1 on v0

v1 whole, which is shorter than its diff:
```python
import jax
import jax.numpy as jnp
from jax import lax
from jax.experimental import pallas as pl
from jax.experimental.pallas import tpu as pltpu
from jax.sharding import Mesh
from jax.sharding import PartitionSpec as P

D = 1280
HEAD = 64
L = 1024
ROWS = 128
AXES = ("zl", "x", "c", "zh", "y")
DP = ("zl", "x", "c")
MP = ("zh", "y")
MESH = pl.DeviceIdType.MESH
BF = jnp.bfloat16
F32 = jnp.float32
NT = (((1,), (1,)), ((), ()))


def lookup(steps, table):
    match = steps[:, None] == jnp.arange(table.shape[0], dtype=jnp.int32)[None, :]
    return jnp.sum(jnp.where(match, table[None, :], jnp.zeros((), table.dtype)), axis=1)


def normed(values, gain):
    wide = values.astype(F32)
    center = wide - jnp.mean(wide, axis=-1, keepdims=True)
    spread = jnp.mean(center * center, axis=-1, keepdims=True)
    return (center * lax.rsqrt(spread + 1e-05) * gain).astype(BF)


def kernel(
    clean, noise, scal, gains, keep, give,
    den, loss,
    recv, qs, wt, qw, w1, w2, n1, qkv, mo, mx, n2, hid, fs, ffin, noised, resid, l1, l2, l3,
    ss, rs, ls,
):
    zl, x, c, zh, y = (lax.axis_index(a) for a in AXES)
    z = zh * 4 + zl
    sends = []
    count = [0]

    def other(name, k, n):
        return {name: lax.rem(lax.axis_index(name) + k, n)}

    def zto(k):
        t = lax.rem(z + k + 8, 8)
        return {"zh": t // 4, "zl": lax.rem(t, 4)}

    def start(src, dst, dev):
        i = count[0]
        count[0] += 1
        d = pltpu.make_async_remote_copy(
            src_ref=src, dst_ref=dst, send_sem=ss.at[i], recv_sem=rs.at[i],
            device_id=dev, device_id_type=MESH,
        )
        d.start()
        sends.append(d)
        return d

    def arrived(ds):
        for d in ds:
            d.wait_recv()

    ys = [other("y", k, 4) for k in (1, 3, 2)]
    xs = [other("x", k, 4) for k in (1, 3, 2)]
    sib = {"c": 1 - c}
    mpg = []
    for k in range(1, 8):
        m = lax.rem(zh * 4 + y + k, 8)
        mpg.append({"zh": m // 4, "y": lax.rem(m, 4)})
    xcg = []
    for k in range(1, 8):
        m = lax.rem(x * 2 + c + k, 8)
        xcg.append({"x": m // 2, "c": lax.rem(m, 2)})
    zlg = [other("zl", k, 4) for k in (1, 2, 3)]

    barrier = pltpu.get_barrier_semaphore()
    greet = mpg + xcg + zlg + [zto(1), zto(-1)]
    for d in greet:
        pl.semaphore_signal(barrier, 1, device_id=d, device_id_type=MESH)
    pl.semaphore_wait(barrier, len(greet))

    s0 = start(give, recv, sib)

    alpha = scal[0:1, 0:1]
    sigma = scal[1:2, 0:1]
    weight = scal[2:3, 0:1]
    noised[...] = (alpha * clean[...].astype(F32) + sigma * noise[...].astype(F32)).astype(BF)
    me = zh * 4 + y
    n1[me] = normed(noised[...], gains[0:1, :])
    tz = start(n1.at[me], n1.at[me], {"zh": 1 - zh})
    ty = [start(n1.at[me], n1.at[me], d) for d in ys]

    arrived([s0])
    mine = keep[...].astype(F32)
    theirs = recv[...].astype(F32)
    first = jnp.where(c == 0, mine, theirs)
    second = jnp.where(c == 0, theirs, mine)
    slab = jnp.concatenate([first, second], axis=0).astype(BF)
    qs[0] = slab[:, 0:128]
    qs[1] = slab[:, 128:256]
    w2[c, zh, zl, x] = slab[:, 896:1536]
    par = lax.rem(y, 2)
    ydst = 2 * zh + y // 2
    lane = pl.multiple_of(par * 128, 128)
    qsend = []
    base = count[0]
    count[0] += 2
    for h in range(2):
        here = jnp.logical_and(zh == h, y == ydst)
        dst = qw.at[c, h, zl, x, :, pl.ds(lane, 128)]
        away = pltpu.make_async_remote_copy(
            src_ref=qs.at[h], dst_ref=dst, send_sem=ss.at[base + h], recv_sem=rs.at[base + par],
            device_id={"zh": h, "y": ydst}, device_id_type=MESH,
        )
        local = pltpu.make_async_copy(qs.at[h], dst, ls)
        qsend.append((here, away, local))

        @pl.when(here)
        def _():
            local.start()

        @pl.when(jnp.logical_not(here))
        def _():
            away.start()

    @pl.when(c == 0)
    def _():
        wt[y] = slab[:, 256:512]

    @pl.when(c == 1)
    def _():
        w1[1, zh, zl, x] = slab[:, 256:896]

    wbase = count[0]
    count[0] += 3
    wy = [
        pltpu.make_async_remote_copy(
            src_ref=wt.at[y], dst_ref=wt.at[y], send_sem=ss.at[wbase + i],
            recv_sem=rs.at[wbase + i], device_id=d, device_id_type=MESH,
        )
        for i, d in enumerate(ys)
    ]

    @pl.when(c == 0)
    def _():
        for d in wy:
            d.start()

    def slab2(k):
        t = lax.rem(z + k + 8, 8)
        return t // 4, lax.rem(t, 4)

    own2 = w2.at[c, zh, zl, x]
    x2 = [start(own2, own2, d) for d in xs]

    homes = (jnp.logical_and(zh == 0, y == 0), jnp.logical_and(zh == 1, y == 3))
    alone = jnp.logical_or(*homes)
    for p in range(2):
        landed = pltpu.make_async_remote_copy(
            src_ref=qs.at[0], dst_ref=qw.at[c, zh, zl, x, :, pl.ds(p * 128, 128)],
            send_sem=ss.at[base], recv_sem=rs.at[base + p], device_id=sib, device_id_type=MESH,
        )
        self_slot = jnp.logical_and(alone, par == p)

        @pl.when(jnp.logical_not(self_slot))
        def _():
            landed.wait_recv()

    for here, away, local in qsend:

        @pl.when(here)
        def _():
            local.wait()

    def ring(ref, k, forward):
        a, b = slab2(-(k - 1) if forward else k - 1)
        return start(ref(a, b), ref(a, b), zto(1 if forward else -1))

    def q_ref(a, b):
        return qw.at[c, a, b, x]

    def w1_ref(a, b):
        return w1.at[c, a, b, x]

    def w2_ref(a, b):
        return w2.at[c, a, b]

    qf = ring(q_ref, 1, True)
    qb = ring(q_ref, 1, False)

    @pl.when(c == 0)
    def _():
        for d in wy:
            d.wait_recv()
        parts = [wt[j][:, 0:160].astype(F32) for j in range(4)]
        w1[0, zh, zl, x] = jnp.concatenate(parts, axis=1).astype(BF)

    x1 = []

    def spread1(k):
        r = w1_ref(*slab2(k))
        for d in xs:
            x1.append(start(r, r, d))

    f1 = ring(w1_ref, 1, True)
    b1 = ring(w1_ref, 1, False)
    spread1(0)

    arrived([qf, qb])
    qf = ring(q_ref, 2, True)
    qb = ring(q_ref, 2, False)
    arrived([qf, qb])
    qf = ring(q_ref, 3, True)
    qb = ring(q_ref, 3, False)
    arrived([f1, b1])
    f1 = ring(w1_ref, 2, True)
    b1 = ring(w1_ref, 2, False)
    spread1(-1)
    spread1(1)
    arrived([qf, qb])
    qf = ring(q_ref, 4, True)
    arrived([qf])
    xq = [start(qw.at[c, :, :, x], qw.at[c, :, :, x], d) for d in xs]

    arrived([f1, b1])
    f1 = ring(w1_ref, 3, True)
    b1 = ring(w1_ref, 3, False)
    spread1(-2)
    spread1(2)

    arrived([tz])
    far = (1 - zh) * 4 + y
    tfy = [start(n1.at[far], n1.at[far], d) for d in ys]

    arrived(x2)
    f2 = ring(w2_ref, 1, True)
    b2 = ring(w2_ref, 1, False)

    arrived([f1, b1])
    f1 = ring(w1_ref, 4, True)
    spread1(-3)
    spread1(3)

    arrived(xq)
    sq = start(qw.at[c], qw.at[c], sib)
    arrived(ty)
    arrived([sq])

    def project(half):
        rows = pl.ds(pl.multiple_of(half * 512, 512), 512)
        tokens = n1[pl.ds(half * 4, 4)].reshape(512, D)
        for t in range(4):
            w = qw[t // 2, t % 2].reshape(D, 256)
            out = jnp.dot(tokens, w, preferred_element_type=F32)
            qkv[t, rows] = out.astype(BF)

    project(zh)
    arrived([f1])
    spread1(-4)
    arrived([f2, b2])
    f2 = ring(w2_ref, 2, True)
    b2 = ring(w2_ref, 2, False)
    arrived(tfy)
    project(1 - zh)

    qrows = pl.multiple_of(zh * 512, 512)

    def pick(rows, spots):
        parts = [qkv[t, rows, a : a + n] for t, a, n in spots]
        if len(parts) == 1:
            return parts[0]
        return jnp.concatenate([p.astype(F32) for p in parts], axis=1).astype(BF)

    heads = (
        ([(0, 0, 64)], [(0, 64, 64)], [(2, 0, 64)]),
        ([(1, 0, 64)], [(1, 64, 64)], [(2, 64, 64)]),
        (
            [(3, 0, 32), (3, 128, 32)],
            [(3, 32, 32), (3, 160, 32)],
            [(3, 64, 32), (3, 192, 32)],
        ),
        ([(0, 128, 64)], [(0, 192, 64)], [(2, 128, 64)]),
        ([(1, 128, 64)], [(1, 192, 64)], [(2, 192, 64)]),
    )

    def attend(n):
        q_at, k_at, v_at = heads[n]
        keys = pick(pl.ds(0, L), k_at)
        values = pick(pl.ds(0, L), v_at)

        def tile(i, carry):
            r = pl.multiple_of(qrows + i * 128, 128)
            q = pick(pl.ds(r, 128), q_at) * BF(HEAD ** (-0.5))
            s = lax.dot_general(q, keys, NT, preferred_element_type=F32)
            p = jnp.exp(s - jnp.max(s, axis=1, keepdims=True))
            total = jnp.sum(p, axis=1, keepdims=True)
            o = jnp.dot(p.astype(BF), values, preferred_element_type=F32) / total
            mo[i, :, n * 64 : n * 64 + 64] = o.astype(BF)
            return carry

        lax.fori_loop(0, 4, tile, 0)

    attend(0)
    attend(1)
    arrived([f2, b2])
    f2 = ring(w2_ref, 3, True)
    b2 = ring(w2_ref, 3, False)
    attend(2)
    attend(3)
    attend(4)

    ax = []
    for k, d in zip((1, 3, 2), ys):
        to = lax.rem(y + k, 4)
        ax.append(start(mo.at[to], mx.at[y], d))
    mx[y] = mo[y]
    arrived([f2, b2])
    f2 = ring(w2_ref, 4, True)
    arrived(x1)
    s1 = start(w1.at[c], w1.at[c], sib)
    arrived(ax)
    arrived([s1])

    cols = []
    for h in range(2):
        acc = None
        for g in range(4):
            w = w1[0, h, g].reshape(320, 640)
            part = jnp.dot(mx[g][:, 0:320], w, preferred_element_type=F32)
            acc = part if acc is None else acc + part
        cols.append(acc)
    resid[...] = (noised[...].astype(F32) + jnp.concatenate(cols, axis=1)).astype(BF)
    n2[y] = normed(resid[...], gains[1:2, :])
    gy = [start(n2.at[y], n2.at[y], d) for d in ys]
    arrived([f2])
    s2 = start(w2.at[c], w2.at[c], sib)
    arrived(gy)
    arrived([s2])

    tokens = n2[...].reshape(512, D)
    for h in range(2):

        def hidden(i, carry):
            at = pl.ds(pl.multiple_of(i * 128, 128), 128)
            g = w2[0, h, :, :, :, at].reshape(D, 128)
            v = w1[1, h, :, :, :, at].reshape(D, 128)
            both = jnp.dot(
                tokens, jnp.concatenate([g, v], axis=1), preferred_element_type=F32
            )
            gate = both[:, 0:128]
            act = 0.5 * gate * (1.0 + lax.erf(gate * 0.5**0.5)) * both[:, 128:256]
            hid[h, :, at] = act.astype(BF)
            return carry

        lax.fori_loop(0, 5, hidden, 0)

    ry = []
    for n in range(5):
        acc = None
        for h in range(2):
            w = w2[1, h].reshape(D, 640)[n * 256 : n * 256 + 256]
            part = lax.dot_general(hid[h], w, NT, preferred_element_type=F32)
            acc = part if acc is None else acc + part
        fs[:, :, n * 256 : n * 256 + 256] = acc.astype(BF).reshape(4, ROWS, 256)
    for k, d in zip((1, 3, 2), ys):
        to = lax.rem(y + k, 4)
        ry.append(start(fs.at[to], ffin.at[y], d))
    ffin[y] = fs[y]
    arrived(ry)
    prediction = resid[...].astype(F32)
    for j in range(4):
        prediction = prediction + ffin[j].astype(F32)
    denoised = (noised[...].astype(F32) - sigma * prediction) / alpha
    den[0] = denoised
    error = denoised - clean[...].astype(F32)
    rowsum = jnp.sum(error * error, axis=1, keepdims=True)
    term = jnp.sum(rowsum, axis=0, keepdims=True) * weight

    def total(buf, slot, group, value):
        buf[slot] = jnp.broadcast_to(value, (8, 128))
        arrived([start(buf.at[slot], buf.at[slot], d) for d in group])
        out = buf[0]
        for j in range(1, len(group) + 1):
            out = out + buf[j]
        return out

    term = total(l1, me, mpg, term)
    term = total(l2, x * 2 + c, xcg, term)
    term = total(l3, zl, zlg, term)
    loss[...] = term

    for d in sends:
        d.wait_send()
    for here, away, local in qsend:

        @pl.when(jnp.logical_not(here))
        def _():
            away.wait_send()

    @pl.when(c == 0)
    def _():
        for d in wy:
            d.wait_send()


N_COPIES = 112


def shards(
    clean, noise, tsteps, alpha_tab, weight_tab, norm1_gain, norm2_gain,
    wqkv, wout, wgate, wvalue, wdown,
):
    alpha = lookup(tsteps, alpha_tab)
    sigma = jnp.sqrt(1.0 - alpha * alpha)
    weight = lookup(tsteps, weight_tab) / (L * D)
    scal = jnp.concatenate([alpha, sigma, weight, jnp.zeros((5,), F32)])
    scal = jnp.broadcast_to(scal[:, None], (8, 128))
    gains = jnp.stack([norm1_gain, norm2_gain])

    even = lax.rem(lax.axis_index("y"), 2) == 0
    first = lax.axis_index("c") == 0
    h_a = jnp.where(even, wqkv[:, :, 0:64], wqkv[:, :, 32:96])
    h_b = jnp.where(even, wqkv[:, :, 64:128], wqkv[:, :, 96:160])
    h_s = jnp.where(even, wqkv[:, :, 128:160], wqkv[:, :, 0:32])
    rows = wout.shape[0]
    t0 = [h_a[0], h_a[1]]
    t1 = [h_b[0], h_b[1]]
    t2 = [h_a[2], h_b[2]]
    t3 = [h_s[0], h_s[1], h_s[2], jnp.zeros((rows, 32), BF)]
    pad = jnp.zeros((rows, 480), BF)
    for_0 = jnp.concatenate(t0 + t1 + [wout, pad, wgate], axis=1)
    for_1 = jnp.concatenate(t2 + t3 + [wvalue, wdown.T], axis=1)
    keep = jnp.where(first, for_0, for_1)
    give = jnp.where(first, for_1, for_0)

    vm = pl.BlockSpec(memory_space=pltpu.VMEM)
    den, loss = pl.pallas_call(
        kernel,
        out_shape=(
            jax.ShapeDtypeStruct((1, ROWS, D), F32),
            jax.ShapeDtypeStruct((8, 128), F32),
        ),
        in_specs=[vm] * 6,
        out_specs=(vm, vm),
        scratch_shapes=[
            pltpu.VMEM((40, 1536), BF),
            pltpu.VMEM((2, 80, 128), BF),
            pltpu.VMEM((4, 80, 256), BF),
            pltpu.VMEM((2, 2, 4, 4, 80, 256), BF),
            pltpu.VMEM((2, 2, 4, 4, 80, 640), BF),
            pltpu.VMEM((2, 2, 4, 4, 80, 640), BF),
            pltpu.VMEM((8, ROWS, D), BF),
            pltpu.VMEM((4, L, 256), BF),
            pltpu.VMEM((4, ROWS, 384), BF),
            pltpu.VMEM((4, ROWS, 384), BF),
            pltpu.VMEM((4, ROWS, D), BF),
            pltpu.VMEM((2, 512, 640), BF),
            pltpu.VMEM((4, ROWS, D), BF),
            pltpu.VMEM((4, ROWS, D), BF),
            pltpu.VMEM((ROWS, D), BF),
            pltpu.VMEM((ROWS, D), BF),
            pltpu.VMEM((8, 8, 128), F32),
            pltpu.VMEM((8, 8, 128), F32),
            pltpu.VMEM((4, 8, 128), F32),
            pltpu.SemaphoreType.DMA((N_COPIES,)),
            pltpu.SemaphoreType.DMA((N_COPIES,)),
            pltpu.SemaphoreType.DMA,
        ],
        compiler_params=pltpu.CompilerParams(
            collective_id=0, has_side_effects=True, vmem_limit_bytes=60 * 2**20
        ),
    )(clean[0], noise[0], scal, gains, keep, give)
    return den, loss[0, 0]


def solution(mesh):
    split = Mesh(mesh.devices.reshape(4, 4, 2, 2, 4), AXES)
    in_specs = (
        P(DP, MP, None), P(DP, MP, None), P(DP), P(), P(), P(), P(),
        P(None, DP, MP), P(DP, MP), P(DP, MP), P(DP, MP), P(MP, DP),
    )
    out_specs = (P(DP, MP, None), P())
    return jax.shard_map(
        shards, mesh=split, in_specs=in_specs, out_specs=out_specs, check_vma=False
    )
```

time: 536 us -> 160 us (0.30)
  waiting for transfers between devices: 313 us -> 0 us
  Pallas kernels: 0 us -> 148 us
  blocking collectives: 128 us -> 0 us
  matrix products: 40.3 us -> 0 us
  local copies, waits for them, and re-layouts: 23.1 us -> 5.59 us
  between operations: 17.5 us -> 3.23 us
    all_gather x4 -> x0, waiting for transfers between devices: 152 us -> none  [the longest x1 82.6 us: shards(): ff_in = lax.all_gather(normed2, MP, axis=1, tiled=True)]
    pallas_call x0 -> x1, Pallas kernels: none -> 148 us  [shards(): pl.pallas_call(kernel, out_shape=(jax.ShapeDtypeStruct((1, ROWS, D), F32)...]
    all_to_all x1 -> x0, waiting for transfers between devices: 94 us -> none  [copy_for_each(): lax.all_to_all(jnp.broadcast_to(value[None], (length, *value.shape)), axi...]
    all_to_all x5 -> x0, blocking collectives: 86.8 us -> none  [copy_for_each(): lax.all_to_all(jnp.broadcast_to(value[None], (length, *value.shape)), axi...]
    reduce_scatter x2 -> x0, waiting for transfers between devices: 67.1 us -> none  [sum_in_order(): blocks = lax.psum_scatter(blocks, axes[k], scatter_dimension=0, tiled=True)]
    psum x5 -> x0, blocking collectives: 41.4 us -> none  [by_axis(): value = lax.psum(value, axis)]
    dot_general x5 -> x0, matrix products: 31 us -> none  [the longest x1 12.9 us: shards(): jnp.dot(hidden, whole_of(wdown, (('dp_0', 'dp_1'), 'dp_2'), 1), preferred...]
    split x3 -> x0, local copies, waits for them, and re-layouts: 11.6 us -> none  [sent_together(): jnp.split(lax.all_gather(both, axis, axis=dim, tiled=True), ends, axis=al...]
  transfers between devices with their start and end apart: 7 -> 0, of which waited for: 5 -> 0; matrix products, arithmetic and copies ran while one was open for 7% -> 0% of each run, Pallas kernels for 0% -> 0%
where the time goes in v1:
time: 160 us
  Pallas kernels  148 us (92%)
  local copies, waits for them, and re-layouts  5.59 us (3%)
  other arithmetic  3.37 us (2%)
  between operations  3.23 us (2%)
    pallas_call x1, Pallas kernels, shards(): pl.pallas_call(kernel, out_shape=(jax.ShapeDtypeStruct((1, ROWS, D), F32)...  148 us
    unnamed x15, local copies, waits for them, and re-layouts  3.51 us

profile of v1, /device:TPU:1, one launch (start us, length us, event | category | flops | bytes accessed | tf_op | source)
XLA Modules:
  0.0 159.9 jit_solution(3399883470045249310)
XLA Ops:
  0.6 0.0 copy-start
  1.3 1.3 select_reduce_fusion
  3.7 0.0 copy-start.5
  4.5 0.6 pad_maximum_fusion.1
  5.1 0.0 copy-start.6
  5.1 0.7 broadcast_in_dim.12.scal
  5.7 0.0 copy-done.5
  5.8 0.0 copy-done.6
  5.8 0.6 pad_maximum_fusion.gains
  6.4 0.0 copy-done
  6.4 0.1 slice_select_fusion.1
  6.5 0.0 copy-start.1
  6.5 0.0 copy-start.2
  6.6 0.8 copy-done.1
  7.3 0.0 copy-done.2
  7.4 0.0 copy-start.3
  7.4 0.1 concatenate.11
  7.5 0.0 copy-start.4
  7.5 0.7 copy-done.3
  8.2 0.0 copy-done.4
  8.2 0.1 concatenate.10
  8.3 0.7 broadcast_select_fusion
  9.0 147.7 %shard_map.131 = (f32[1,128,1280]{2,1,0:T(8,128)}, f32[8,128]{1,0:T(8,128)}) custom-call(bf16[128,1280]{1,0:T(8,128)(2,1)} %bitcast.26, bf16[128,1280]{1,0:T(8,128)(2,1)} %bitcast.27, f32[8,128]{1,0:T(8,128)} %broadcast_in_dim.12.scal, f32[2,1280]{1,0:T(2,128)} %pad_maximum_fusion.gains, bf16[40,1536]{1,0:T(8,128)(2,1)} %get-tuple-element.7.keep, ...), custom_call_target="tpu_custom_call" | custom-call | tf_op jit(solution)/shard_map/pallas_call | solution.py:441
  156.8 1.2 slice.63
  157.9 2.0 %copy.16 = f32[1,128,1280]{2,1,0:T(8,128)} copy(f32[1,128,1280]{2,1,0:T(8,128)} %get-tuple-element.26) | data formatting | bytes 1310720
  (8 shorter events, 0.0 us)
Async XLA Ops:
  0.6 5.8 %copy-start = (bf16[3,40,160]{2,1,0:T(8,128)(2,1)S(1)}, bf16[3,40,160]{2,1,0:T(8,128)(2,1)}, u32[]{:S(2)}) copy-start(bf16[3,40,160]{2,1,0:T(8,128)(2,1)} %param.19) | copy-start | bytes 115204
  3.7 2.0 %copy-start.5 = (f32[1280]{0:T(1024)S(1)}, f32[1280]{0:T(1024)}, u32[]{:S(2)}) copy-start(f32[1280]{0:T(1024)} %param.17) | copy-start | bytes 15364
  5.1 0.7 copy-start.6
  6.5 0.8 copy-start.1
  6.5 0.8 copy-start.2
  7.4 0.8 copy-start.3
  7.5 0.7 copy-start.4

commit v2 on v1

v2 whole, which is shorter than its diff:
```python
import jax
import jax.numpy as jnp
from jax import lax
from jax.experimental import pallas as pl
from jax.experimental.pallas import tpu as pltpu
from jax.sharding import Mesh
from jax.sharding import PartitionSpec as P

D = 1280
HEAD = 64
L = 1024
ROWS = 128
AXES = ("zl", "x", "c", "zh", "y")
DP = ("zl", "x", "c")
MP = ("zh", "y")
MESH = pl.DeviceIdType.MESH
BF = jnp.bfloat16
F32 = jnp.float32
NT = (((1,), (1,)), ((), ()))


def normed(values, gain):
    wide = values.astype(F32)
    center = wide - jnp.mean(wide, axis=-1, keepdims=True)
    spread = jnp.mean(center * center, axis=-1, keepdims=True)
    return (center * lax.rsqrt(spread + 1e-05) * gain).astype(BF)


def kernel(
    tsteps, clean, noise, alpha_tab, weight_tab, gain1, gain2, wqkv, wout, wgate, wvalue, wdown,
    den, loss,
    keep, give, recv, qs, wt, qw, w1, w2, n1, qh, kh, vh, mo, mx, n2, hid, fs, ffin, noised, resid,
    l1, l2, ss, rs, ls,
):
    zl, x, c, zh, y = (lax.axis_index(a) for a in AXES)
    z = zh * 4 + zl
    sends = []
    count = [0]

    def other(name, k, n):
        return {name: lax.rem(lax.axis_index(name) + k, n)}

    def zto(k):
        t = lax.rem(z + k + 8, 8)
        return {"zh": t // 4, "zl": lax.rem(t, 4)}

    def make(src, dst, dev):
        i = count[0]
        count[0] += 1
        d = pltpu.make_async_remote_copy(
            src_ref=src, dst_ref=dst, send_sem=ss.at[i], recv_sem=rs.at[i],
            device_id=dev, device_id_type=MESH,
        )
        sends.append(d)
        return d

    def start(src, dst, dev):
        d = make(src, dst, dev)
        d.start()
        return d

    def arrived(ds):
        for d in ds:
            d.wait_recv()

    ys = [other("y", k, 4) for k in (1, 3, 2)]
    xs = [other("x", k, 4) for k in (1, 3, 2)]
    sib = {"c": 1 - c}
    plane = []
    for k in range(1, 16):
        m = lax.rem(x * 4 + y + k, 16)
        plane.append({"x": m // 4, "y": lax.rem(m, 4)})
    column = []
    for k in range(1, 16):
        m = lax.rem(z * 2 + c + k, 16)
        column.append({"zh": m // 8, "zl": lax.rem(m // 2, 4), "c": lax.rem(m, 2)})
    across = [{"zh": 1 - zh, "y": lax.rem(y + k, 4)} for k in (1, 2, 3)]

    barrier = pltpu.get_barrier_semaphore()
    greet = plane + column + across
    for d in greet:
        pl.semaphore_signal(barrier, 1, device_id=d, device_id_type=MESH)

    step = tsteps[0]
    match = lax.broadcasted_iota(jnp.int32, alpha_tab.shape, 1) == step
    alpha = jnp.sum(jnp.where(match, alpha_tab[...], 0.0), axis=1, keepdims=True)
    weight = jnp.sum(jnp.where(match, weight_tab[...], 0.0), axis=1, keepdims=True) / (L * D)
    sigma = jnp.sqrt(1.0 - alpha * alpha)

    par = lax.rem(y, 2)

    def fold(value, mine_at):
        value = value.astype(BF)
        at = pl.ds(mine_at[1], value.shape[1])

        @pl.when(c == mine_at[0])
        def _():
            keep[:, at] = value

        @pl.when(c != mine_at[0])
        def _():
            give[:, at] = value

    wide = [wqkv[j].astype(F32) for j in range(3)]
    h_a = [jnp.where(par == 0, w[:, 0:64], w[:, 32:96]) for w in wide]
    h_b = [jnp.where(par == 0, w[:, 64:128], w[:, 96:160]) for w in wide]
    h_s = [jnp.where(par == 0, w[:, 128:160], w[:, 0:32]) for w in wide]
    fold(jnp.concatenate([h_a[0], h_a[1]], axis=1), (0, 0))
    fold(jnp.concatenate([h_b[0], h_b[1]], axis=1), (0, 128))
    fold(jnp.concatenate([h_a[2], h_b[2]], axis=1), (1, 0))
    fold(jnp.concatenate(h_s + [jnp.zeros((40, 32), F32)], axis=1), (1, 128))
    fold(jnp.concatenate([wout[...].astype(F32), jnp.zeros((40, 96), F32)], axis=1), (0, 256))
    fold(wvalue[...], (1, 256))
    fold(wgate[...], (0, 896))
    fold(wdown[...].astype(F32).T, (1, 896))

    noised[...] = (alpha * clean[...].astype(F32) + sigma * noise[...].astype(F32)).astype(BF)
    me = zh * 4 + y
    n1[me] = normed(noised[...], gain1[...])

    pl.semaphore_wait(barrier, len(greet))
    s0 = start(give, recv, sib)
    tz = start(n1.at[me], n1.at[me], {"zh": 1 - zh})

    def spread_y(ref):
        return [start(ref(y), ref(y), d) for d in ys[:2]]

    def relay_y(ref):
        low, high = pl.ds(0, 64), pl.ds(64, 64)
        a, b = ref(lax.rem(y + 3, 4)).at[low], ref(lax.rem(y + 1, 4)).at[high]
        return [start(a, a, ys[0]), start(b, b, ys[1])]

    def near(j):
        return n1.at[zh * 4 + j]

    def far(j):
        return n1.at[(1 - zh) * 4 + j]

    ty = spread_y(near)

    arrived([s0])
    mine = keep[...].astype(F32)
    theirs = recv[...].astype(F32)
    first = jnp.where(c == 0, mine, theirs)
    second = jnp.where(c == 0, theirs, mine)
    slab = jnp.concatenate([first, second], axis=0).astype(BF)
    qs[0] = slab[:, 0:128]
    qs[1] = slab[:, 128:256]
    w2[c, zh, zl, x] = slab[:, 896:1536]
    ydst = 2 * zh + y // 2
    lane = pl.multiple_of(par * 128, 128)
    qsend = []
    base = count[0]
    count[0] += 2
    for h in range(2):
        here = jnp.logical_and(zh == h, y == ydst)
        dst = qw.at[c, h, zl, x, :, pl.ds(lane, 128)]
        away = pltpu.make_async_remote_copy(
            src_ref=qs.at[h], dst_ref=dst, send_sem=ss.at[base + h], recv_sem=rs.at[base + par],
            device_id={"zh": h, "y": ydst}, device_id_type=MESH,
        )
        local = pltpu.make_async_copy(qs.at[h], dst, ls)
        qsend.append((here, away, local))

        @pl.when(here)
        def _():
            local.start()

        @pl.when(jnp.logical_not(here))
        def _():
            away.start()

    @pl.when(c == 0)
    def _():
        wt[y] = slab[:, 256:512]

    @pl.when(c == 1)
    def _():
        w1[1, zh, zl, x] = slab[:, 256:896]

    wbase = count[0]
    count[0] += 3
    wy = [
        pltpu.make_async_remote_copy(
            src_ref=wt.at[y], dst_ref=wt.at[y], send_sem=ss.at[wbase + i],
            recv_sem=rs.at[wbase + i], device_id=d, device_id_type=MESH,
        )
        for i, d in enumerate(ys)
    ]

    @pl.when(c == 0)
    def _():
        for d in wy:
            d.start()

    def slab2(k):
        t = lax.rem(z + k + 8, 8)
        return t // 4, lax.rem(t, 4)

    own2 = w2.at[c, zh, zl, x]
    x2 = [start(own2, own2, d) for d in xs]

    homes = (jnp.logical_and(zh == 0, y == 0), jnp.logical_and(zh == 1, y == 3))
    alone = jnp.logical_or(*homes)
    for p in range(2):
        landed = pltpu.make_async_remote_copy(
            src_ref=qs.at[0], dst_ref=qw.at[c, zh, zl, x, :, pl.ds(p * 128, 128)],
            send_sem=ss.at[base], recv_sem=rs.at[base + p], device_id=sib, device_id_type=MESH,
        )
        self_slot = jnp.logical_and(alone, par == p)

        @pl.when(jnp.logical_not(self_slot))
        def _():
            landed.wait_recv()

    for here, away, local in qsend:

        @pl.when(here)
        def _():
            local.wait()

    def hop(ref, k, forward):
        a, b = slab2(-(k - 1) if forward else k - 1)
        return make(ref(a, b), ref(a, b), zto(1 if forward else -1))

    def ring(ref, k, forward):
        d = hop(ref, k, forward)
        d.start()
        return d

    def q_ref(a, b):
        return qw.at[c, a, b, x]

    def w1_ref(a, b):
        return w1.at[c, a, b, x]

    def w2_ref(a, b):
        return w2.at[c, a, b]

    qf = ring(q_ref, 1, True)
    qb = ring(q_ref, 1, False)

    @pl.when(c == 0)
    def _():
        for d in wy:
            d.wait_recv()
        parts = [wt[j][:, 0:160].astype(F32) for j in range(4)]
        w1[0, zh, zl, x] = jnp.concatenate(parts, axis=1).astype(BF)

    x1 = []

    def spread1(k):
        r = w1_ref(*slab2(k))
        for d in xs:
            x1.append(start(r, r, d))

    f1 = ring(w1_ref, 1, True)
    b1 = ring(w1_ref, 1, False)
    spread1(0)

    arrived([qf, qb])
    qf = ring(q_ref, 2, True)
    qb = ring(q_ref, 2, False)
    arrived(ty)
    ty = relay_y(near)
    arrived([qf, qb])
    qf = ring(q_ref, 3, True)
    qb = ring(q_ref, 3, False)
    arrived([f1, b1])
    f1 = ring(w1_ref, 2, True)
    b1 = ring(w1_ref, 2, False)
    spread1(-1)
    spread1(1)
    arrived([qf, qb])
    qf = ring(q_ref, 4, True)
    arrived([qf])
    xq = [start(qw.at[c, :, :, x], qw.at[c, :, :, x], d) for d in xs]
    arrived([tz])
    tf = spread_y(far)

    arrived([f1, b1])
    f1 = ring(w1_ref, 3, True)
    b1 = ring(w1_ref, 3, False)
    spread1(-2)
    spread1(2)

    arrived(x2)
    f2 = ring(w2_ref, 1, True)
    b2 = ring(w2_ref, 1, False)

    arrived(xq)
    sq = start(qw.at[c], qw.at[c], sib)
    arrived(ty)
    arrived(tf)
    tf = relay_y(far)

    arrived([f1, b1])
    f1 = ring(w1_ref, 4, True)
    spread1(-3)
    spread1(3)
    arrived([sq])

    def project(half):
        rows = pl.ds(pl.multiple_of(half * 512, 512), 512)
        tokens = n1[pl.ds(half * 4, 4)].reshape(512, D)

        def out(t):
            w = qw[t // 2, t % 2].reshape(D, 256)
            return jnp.dot(tokens, w, preferred_element_type=F32)

        def put(ref, n, value):
            ref[n, rows] = value.astype(BF)

        for t, heads in ((0, (0, 3)), (1, (1, 4))):
            o = out(t)
            for j, n in enumerate(heads):
                put(qh, n, o[:, j * 128 : j * 128 + 64] * HEAD ** (-0.5))
                put(kh, n, o[:, j * 128 + 64 : j * 128 + 128])
        o = out(2)
        for j, n in enumerate((0, 1, 3, 4)):
            put(vh, n, o[:, j * 64 : j * 64 + 64])
        o = out(3)
        halves = [
            jnp.concatenate([o[:, j : j + 32], o[:, j + 128 : j + 160]], axis=1)
            for j in (0, 32, 64)
        ]
        put(qh, 2, halves[0] * HEAD ** (-0.5))
        put(kh, 2, halves[1])
        put(vh, 2, halves[2])

    project(zh)
    arrived([f1])
    spread1(-4)
    arrived([f2, b2])
    f2 = ring(w2_ref, 2, True)
    b2 = ring(w2_ref, 2, False)
    arrived(tf)
    project(1 - zh)

    held = [f2, b2]
    f2 = hop(w2_ref, 3, True)
    b2 = hop(w2_ref, 3, False)
    abase = count[0]
    count[0] += 3

    def give_tile(t, i):
        return pltpu.make_async_remote_copy(
            src_ref=mo.at[i], dst_ref=mx.at[y], send_sem=ss.at[abase + t],
            recv_sem=rs.at[abase + t], device_id={"y": i}, device_id_type=MESH,
        )

    def attend(t, carry):
        i = lax.rem(y + t + 1, 4)
        r = pl.ds(pl.multiple_of(zh * 512 + i * 128, 128), 128)

        @pl.when(t == 2)
        def _():
            arrived(held)
            f2.start()
            b2.start()

        for n in range(5):
            s = lax.dot_general(qh[n, r], kh[n], NT, preferred_element_type=F32)
            p = jnp.exp(s - jnp.max(s, axis=1, keepdims=True))
            total = jnp.sum(p, axis=1, keepdims=True)
            o = jnp.dot(p.astype(BF), vh[n], preferred_element_type=F32) / total
            mo[i, :, n * 64 : n * 64 + 64] = o.astype(BF)

        @pl.when(t < 3)
        def _():
            give_tile(t, i).start()

        return carry

    lax.fori_loop(0, 4, attend, 0)
    ax = [give_tile(t, lax.rem(y + t + 1, 4)) for t in range(3)]
    sends.extend(ax)

    arrived([f2, b2])
    f2 = ring(w2_ref, 4, True)
    arrived(x1)
    s1 = start(w1.at[c], w1.at[c], sib)
    mx[y] = mo[y]
    arrived(ax)
    arrived([s1])

    cols = []
    for h in range(2):
        acc = None
        for g in range(4):
            w = w1[0, h, g].reshape(320, 640)
            part = jnp.dot(mx[g][:, 0:320], w, preferred_element_type=F32)
            acc = part if acc is None else acc + part
        cols.append(acc)
    resid[...] = (noised[...].astype(F32) + jnp.concatenate(cols, axis=1)).astype(BF)
    n2[y] = normed(resid[...], gain2[...])

    def block(j):
        return n2.at[j]

    gy = spread_y(block)
    arrived([f2])
    s2 = start(w2.at[c], w2.at[c], sib)
    arrived([s2])

    def feed(blocks, ship):
        m = ROWS * len(blocks)
        tokens = jnp.concatenate([n2[j] for j in blocks], axis=0) if m > ROWS else n2[blocks[0]]
        for h in range(2):

            def hidden(i, carry):
                at = pl.ds(pl.multiple_of(i * 128, 128), 128)
                g = w2[0, h, :, :, :, at].reshape(D, 128)
                v = w1[1, h, :, :, :, at].reshape(D, 128)
                both = jnp.dot(
                    tokens, jnp.concatenate([g, v], axis=1), preferred_element_type=F32
                )
                gate = both[:, 0:128]
                act = 0.5 * gate * (1.0 + lax.erf(gate * 0.5**0.5)) * both[:, 128:256]
                hid[h, 0:m, at] = act.astype(BF)
                return carry

            lax.fori_loop(0, 5, hidden, 0)
        copies = []
        for n in range(5):
            acc = None
            for h in range(2):
                w = w2[1, h].reshape(D, 640)[n * 256 : n * 256 + 256]
                part = lax.dot_general(hid[h, 0:m], w, NT, preferred_element_type=F32)
                acc = part if acc is None else acc + part
            at = pl.ds(n * 256, 256)
            for q, j in enumerate(blocks):
                part = acc[q * ROWS : q * ROWS + ROWS].astype(BF)
                if ship:
                    fs[j, :, at] = part
                    copies.append(start(fs.at[j, :, at], ffin.at[y, :, at], {"y": j}))
                else:
                    ffin[j, :, at] = part
        return copies

    feed([y], False)
    arrived(gy)
    gy = relay_y(block)
    ry = feed([lax.rem(y + 1, 4), lax.rem(y + 3, 4)], True)
    arrived(gy)
    ry += feed([lax.rem(y + 2, 4)], True)
    arrived(ry)
    prediction = resid[...].astype(F32)
    for j in range(4):
        prediction = prediction + ffin[j].astype(F32)
    denoised = (noised[...].astype(F32) - sigma * prediction) / alpha
    den[0] = denoised
    error = denoised - clean[...].astype(F32)
    rowsum = jnp.sum(error * error, axis=1, keepdims=True)
    term = jnp.sum(rowsum, axis=0, keepdims=True) * weight

    def total(buf, slot, group, value):
        buf[slot] = jnp.broadcast_to(value, (8, 128))
        arrived([start(buf.at[slot], buf.at[slot], d) for d in group])
        out = buf[0]
        for j in range(1, len(group) + 1):
            out = out + buf[j]
        return out

    term = total(l1, x * 4 + y, plane, term)
    term = total(l2, z * 2 + c, column, term)
    loss[...] = term

    for d in sends:
        d.wait_send()
    for here, away, local in qsend:

        @pl.when(jnp.logical_not(here))
        def _():
            away.wait_send()

    @pl.when(c == 0)
    def _():
        for d in wy:
            d.wait_send()


N_COPIES = 144


def shards(
    clean, noise, tsteps, alpha_tab, weight_tab, norm1_gain, norm2_gain,
    wqkv, wout, wgate, wvalue, wdown,
):
    vm = pl.BlockSpec(memory_space=pltpu.VMEM)
    den, loss = pl.pallas_call(
        kernel,
        out_shape=(
            jax.ShapeDtypeStruct((1, ROWS, D), F32),
            jax.ShapeDtypeStruct((8, 128), F32),
        ),
        in_specs=[pl.BlockSpec(memory_space=pltpu.SMEM)] + [vm] * 11,
        out_specs=(vm, vm),
        scratch_shapes=[
            pltpu.VMEM((40, 1536), BF),
            pltpu.VMEM((40, 1536), BF),
            pltpu.VMEM((40, 1536), BF),
            pltpu.VMEM((2, 80, 128), BF),
            pltpu.VMEM((4, 80, 256), BF),
            pltpu.VMEM((2, 2, 4, 4, 80, 256), BF),
            pltpu.VMEM((2, 2, 4, 4, 80, 640), BF),
            pltpu.VMEM((2, 2, 4, 4, 80, 640), BF),
            pltpu.VMEM((8, ROWS, D), BF),
            pltpu.VMEM((5, L, 64), BF),
            pltpu.VMEM((5, L, 64), BF),
            pltpu.VMEM((5, L, 64), BF),
            pltpu.VMEM((4, ROWS, 384), BF),
            pltpu.VMEM((4, ROWS, 384), BF),
            pltpu.VMEM((4, ROWS, D), BF),
            pltpu.VMEM((2, 256, 640), BF),
            pltpu.VMEM((4, ROWS, D), BF),
            pltpu.VMEM((4, ROWS, D), BF),
            pltpu.VMEM((ROWS, D), BF),
            pltpu.VMEM((ROWS, D), BF),
            pltpu.VMEM((16, 8, 128), F32),
            pltpu.VMEM((16, 8, 128), F32),
            pltpu.SemaphoreType.DMA((N_COPIES,)),
            pltpu.SemaphoreType.DMA((N_COPIES,)),
            pltpu.SemaphoreType.DMA,
        ],
        compiler_params=pltpu.CompilerParams(
            collective_id=0, has_side_effects=True, vmem_limit_bytes=60 * 2**20
        ),
    )(
        tsteps, clean[0], noise[0], alpha_tab[None], weight_tab[None], norm1_gain[None],
        norm2_gain[None], wqkv, wout, wgate, wvalue, wdown,
    )
    return den, loss[0, 0]


def solution(mesh):
    split = Mesh(mesh.devices.reshape(4, 4, 2, 2, 4), AXES)
    in_specs = (
        P(DP, MP, None), P(DP, MP, None), P(DP), P(), P(), P(), P(),
        P(None, DP, MP), P(DP, MP), P(DP, MP), P(DP, MP), P(MP, DP),
    )
    out_specs = (P(DP, MP, None), P())
    return jax.shard_map(
        shards, mesh=split, in_specs=in_specs, out_specs=out_specs, check_vma=False
    )
```

time: 160 us -> 154 us (0.963)
  other arithmetic: 3.37 us -> 0 us
  Pallas kernels: 148 us -> 146 us
  between operations: 3.23 us -> 1.32 us
    unnamed x15 -> x6, local copies, waits for them, and re-layouts: 3.51 us -> 3.66 us
where the time goes in v2:
time: 154 us
  Pallas kernels  146 us (95%)
  local copies, waits for them, and re-layouts  6.05 us (4%)
    pallas_call x1, Pallas kernels, shards(): pl.pallas_call(kernel, out_shape=(jax.ShapeDtypeStruct((1, ROWS, D), F32)...  146 us
    unnamed x6, local copies, waits for them, and re-layouts  3.66 us

profile of v2, /device:TPU:1, one launch (start us, length us, event | category | flops | bytes accessed | tf_op | source)
XLA Modules:
  0.0 153.8 jit_solution(14018025702707663540)
XLA Ops:
  0.6 0.0 copy-start
  1.3 0.0 copy-start.1
  1.3 0.0 copy-done
  1.3 0.6 broadcast_in_dim.14.gain1
  1.9 0.1 copy-done.1
  2.0 0.6 broadcast_in_dim.15.gain2
  2.6 1.6 %copy.14.wdown = bf16[640,40]{1,0:T(8,128)(2,1)} copy(bf16[640,40]{0,1:T(8,128)(2,1)} %param.23) | data formatting | bytes 102400 | tf_op args[11]
  4.2 146.4 %shard_map.131 = (f32[1,128,1280]{2,1,0:T(8,128)}, f32[8,128]{1,0:T(8,128)}) custom-call(s32[1]{0:T(128)S(6)} %copy.16.tsteps, bf16[128,1280]{1,0:T(8,128)(2,1)} %bitcast.5, bf16[128,1280]{1,0:T(8,128)(2,1)} %bitcast.6, f32[1,1000]{1,0:T(1,128)} %bitcast.7, f32[1,1000]{1,0:T(1,128)} %bitcast.8, f32[1,1280]{1,0:T(1,128)} %broadcast_in_dim.14.gain1, ...), custom_call_target="tpu_custom_call" | custom-call | tf_op jit(solution)/shard_map/pallas_call | solution.py:491
  150.6 1.2 slice.3
  151.8 2.0 %copy.17 = f32[1,128,1280]{2,1,0:T(8,128)} copy(f32[1,128,1280]{2,1,0:T(8,128)} %get-tuple-element.8) | data formatting | bytes 1310720
Async XLA Ops:
  0.6 0.7 copy-start
  1.3 0.7 copy-start.1

commit v3 on v2

--- a/solution.py
+++ b/solution.py
@@ -29,7 +29,7 @@
 def kernel(
     tsteps, clean, noise, alpha_tab, weight_tab, gain1, gain2, wqkv, wout, wgate, wvalue, wdown,
     den, loss,
-    keep, give, recv, qs, wt, qw, w1, w2, n1, qh, kh, vh, mo, mx, n2, hid, fs, ffin, noised, resid,
+    keep, give, recv, qs, wt, qw, wb, n1, qh, kh, vh, mo, mx, n2, hid, fs, ffin, noised, resid,
     l1, l2, ss, rs, ls,
 ):
     zl, x, c, zh, y = (lax.axis_index(a) for a in AXES)
@@ -112,7 +112,7 @@
     fold(jnp.concatenate([wout[...].astype(F32), jnp.zeros((40, 96), F32)], axis=1), (0, 256))
     fold(wvalue[...], (1, 256))
     fold(wgate[...], (0, 896))
-    fold(wdown[...].astype(F32).T, (1, 896))
+    fold(wdown[...], (1, 896))
 
     noised[...] = (alpha * clean[...].astype(F32) + sigma * noise[...].astype(F32)).astype(BF)
     me = zh * 4 + y
@@ -120,7 +120,6 @@
 
     pl.semaphore_wait(barrier, len(greet))
     s0 = start(give, recv, sib)
-    tz = start(n1.at[me], n1.at[me], {"zh": 1 - zh})
 
     def spread_y(ref):
         return [start(ref(y), ref(y), d) for d in ys[:2]]
@@ -135,8 +134,6 @@
 
     def far(j):
         return n1.at[(1 - zh) * 4 + j]
-
-    ty = spread_y(near)
 
     arrived([s0])
     mine = keep[...].astype(F32)
@@ -146,7 +143,7 @@
     slab = jnp.concatenate([first, second], axis=0).astype(BF)
     qs[0] = slab[:, 0:128]
     qs[1] = slab[:, 128:256]
-    w2[c, zh, zl, x] = slab[:, 896:1536]
+    wb[c, zh, zl, x, :, 640:1280] = slab[:, 896:1536]
     ydst = 2 * zh + y // 2
     lane = pl.multiple_of(par * 128, 128)
     qsend = []
@@ -176,7 +173,7 @@
 
     @pl.when(c == 1)
     def _():
-        w1[1, zh, zl, x] = slab[:, 256:896]
+        wb[1, zh, zl, x, :, 0:640] = slab[:, 256:896]
 
     wbase = count[0]
     count[0] += 3
@@ -197,8 +194,70 @@
         t = lax.rem(z + k + 8, 8)
         return t // 4, lax.rem(t, 4)
 
-    own2 = w2.at[c, zh, zl, x]
+    own2 = wb.at[c, zh, zl, x, :, CUT:1280]
     x2 = [start(own2, own2, d) for d in xs]
+    ty = spread_y(near)
+    tz = []
+
+    def cross(*ks):
+        for k in ks:
+            r = n1.at[me, pl.ds(32 * k, 32)]
+            tz.append(start(r, r, {"zh": 1 - zh}))
+
+    cross(0)
+
+    @pl.when(c == 0)
+    def _():
+        for d in wy:
+            d.wait_recv()
+        parts = [wt[j][:, 0:160].astype(F32) for j in range(4)]
+        wb[0, zh, zl, x, :, 0:640] = jnp.concatenate(parts, axis=1).astype(BF)
+
+    def hop(ref, k, forward):
+        a, b = slab2(-(k - 1) if forward else k - 1)
+        r = ref(a, b, None if k < 4 else 1 - int(forward))
+        return make(r, r, zto(1 if forward else -1))
+
+    def ring(ref, k):
+        ds = [hop(ref, k, True), hop(ref, k, False)]
+        for d in ds:
+            d.start()
+        return ds
+
+    def even_ref(a, b, part):
+        rows = slice(None) if part is None else slice(48 * part, 48 + 32 * part)
+        return qw.at[c, a, b, x, rows, 0:128]
+
+    def odd_ref(a, b, part):
+        which = slice(None) if part is None else slice(2 * part, 2 * part + 2)
+        return qw.at[c, a, b, which, :, 128:256]
+
+    def w1_ref(a, b, part):
+        cols = slice(0, CUT) if part is None else slice(CUT // 2 * part, CUT // 2 * (part + 1))
+        return wb.at[c, a, b, x, :, cols]
+
+    def w2_ref(a, b, part):
+        which = slice(None) if part is None else slice(2 * part, 2 * part + 2)
+        return wb.at[c, a, b, which, :, CUT:1280]
+
+    x1 = {}
+
+    def spread1(*ks):
+        for k in ks:
+            r = w1_ref(*slab2(k), None)
+            x1[k] = [start(r, r, d) for d in xs[:2]]
+
+    x1b = []
+
+    def relay1(*ks):
+        for k in ks:
+            arrived(x1[k])
+            a, b = slab2(k)
+            turn = 1 + 2 * a
+            r = wb.at[c, a, b, lax.rem(x + 4 - turn, 4), :, 0:CUT]
+            x1b.append(start(r, r, {"x": lax.rem(x + turn, 4)}))
+
+    spread1(0)
 
     homes = (jnp.logical_and(zh == 0, y == 0), jnp.logical_and(zh == 1, y == 3))
     alone = jnp.logical_or(*homes)
@@ -219,86 +278,59 @@
         def _():
             local.wait()
 
-    def hop(ref, k, forward):
-        a, b = slab2(-(k - 1) if forward else k - 1)
-        return make(ref(a, b), ref(a, b), zto(1 if forward else -1))
-
-    def ring(ref, k, forward):
-        d = hop(ref, k, forward)
-        d.start()
-        return d
-
-    def q_ref(a, b):
-        return qw.at[c, a, b, x]
-
-    def w1_ref(a, b):
-        return w1.at[c, a, b, x]
-
-    def w2_ref(a, b):
-        return w2.at[c, a, b]
-
-    qf = ring(q_ref, 1, True)
-    qb = ring(q_ref, 1, False)
-
-    @pl.when(c == 0)
-    def _():
-        for d in wy:
-            d.wait_recv()
-        parts = [wt[j][:, 0:160].astype(F32) for j in range(4)]
-        w1[0, zh, zl, x] = jnp.concatenate(parts, axis=1).astype(BF)
-
-    x1 = []
-
-    def spread1(k):
-        r = w1_ref(*slab2(k))
-        for d in xs:
-            x1.append(start(r, r, d))
-
-    f1 = ring(w1_ref, 1, True)
-    b1 = ring(w1_ref, 1, False)
-    spread1(0)
-
-    arrived([qf, qb])
-    qf = ring(q_ref, 2, True)
-    qb = ring(q_ref, 2, False)
+    er = ring(even_ref, 1)
+    cross(1)
+    odd = qw.at[c, zh, zl, x, :, 128:256]
+    ox = [start(odd, odd, d) for d in xs]
+
+    arrived(er)
+    er = ring(even_ref, 2)
+    w1r = ring(w1_ref, 1)
+    arrived(ox)
+    dr = ring(odd_ref, 1)
+    arrived(er)
+    er = ring(even_ref, 3)
+    cross(2)
+    arrived(dr)
+    dr = ring(odd_ref, 2)
+    arrived(er)
+    er = ring(even_ref, 4)
+    cross(3)
+    arrived(w1r)
+    spread1(-1, 1)
     arrived(ty)
     ty = relay_y(near)
-    arrived([qf, qb])
-    qf = ring(q_ref, 3, True)
-    qb = ring(q_ref, 3, False)
-    arrived([f1, b1])
-    f1 = ring(w1_ref, 2, True)
-    b1 = ring(w1_ref, 2, False)
-    spread1(-1)
-    spread1(1)
-    arrived([qf, qb])
-    qf = ring(q_ref, 4, True)
-    arrived([qf])
-    xq = [start(qw.at[c, :, :, x], qw.at[c, :, :, x], d) for d in xs]
-    arrived([tz])
+    arrived(er)
+    ex = [
+        start(qw.at[c, :, :, x, :, 0:128], qw.at[c, :, :, x, :, 0:128], d) for d in xs
+    ]
+    arrived(dr)
+    dr = ring(odd_ref, 3)
+    w1r = ring(w1_ref, 2)
+    relay1(0)
+    arrived(tz)
     tf = spread_y(far)
-
-    arrived([f1, b1])
-    f1 = ring(w1_ref, 3, True)
-    b1 = ring(w1_ref, 3, False)
-    spread1(-2)
-    spread1(2)
-
+    arrived(dr)
+    dr = ring(odd_ref, 4)
+    arrived(w1r)
+    w1r = ring(w1_ref, 3)
+    spread1(-2, 2)
+    arrived(ex)
+    half = qw.at[c, :, :, :, :, 0:128]
+    sq = [start(half, half, sib)]
+    arrived(dr)
+    half = qw.at[c, :, :, :, :, 128:256]
+    sq.append(start(half, half, sib))
+    relay1(-1, 1)
     arrived(x2)
-    f2 = ring(w2_ref, 1, True)
-    b2 = ring(w2_ref, 1, False)
-
-    arrived(xq)
-    sq = start(qw.at[c], qw.at[c], sib)
-    arrived(ty)
+    w2r = ring(w2_ref, 1)
     arrived(tf)
     tf = relay_y(far)
-
-    arrived([f1, b1])
-    f1 = ring(w1_ref, 4, True)
-    spread1(-3)
-    spread1(3)
-    arrived([sq])
+    arrived(w1r)
+    w1r = ring(w1_ref, 4)
+    spread1(-3, 3)
+    arrived(ty)
+    arrived(sq)
 
     def project(half):
         rows = pl.ds(pl.multiple_of(half * 512, 512), 512)
@@ -329,17 +361,16 @@
         put(vh, 2, halves[2])
 
     project(zh)
-    arrived([f1])
-    spread1(-4)
-    arrived([f2, b2])
-    f2 = ring(w2_ref, 2, True)
-    b2 = ring(w2_ref, 2, False)
+    relay1(-2, 2)
     arrived(tf)
     project(1 - zh)
-
-    held = [f2, b2]
-    f2 = hop(w2_ref, 3, True)
-    b2 = hop(w2_ref, 3, False)
+    arrived(w1r)
+    spread1(4)
+    arrived(w2r)
+    w2r = ring(w2_ref, 2)
+
+    held = w2r
+    w2r = [hop(w2_ref, 3, True), hop(w2_ref, 3, False)]
     abase = count[0]
     count[0] += 3
 
@@ -356,8 +387,8 @@
         @pl.when(t == 2)
         def _():
             arrived(held)
-            f2.start()
-            b2.start()
+            for d in w2r:
+                d.start()
 
         for n in range(5):
             s = lax.dot_general(qh[n, r], kh[n], NT, preferred_element_type=F32)
@@ -376,19 +407,28 @@
     ax = [give_tile(t, lax.rem(y + t + 1, 4)) for t in range(3)]
     sends.extend(ax)
 
-    arrived([f2, b2])
-    f2 = ring(w2_ref, 4, True)
-    arrived(x1)
-    s1 = start(w1.at[c], w1.at[c], sib)
     mx[y] = mo[y]
+    arrived(w2r)
+    w2r = ring(w2_ref, 4)
+    relay1(-3, 3, 4)
+
+    def share(k, lo, hi):
+        r = wb.at[c, :, :, lax.rem(x + k, 4), :, lo:hi]
+        return start(r, r, sib)
+
+    s1 = [share(k, 0, 640) for k in (0, 1, 3)]
+    s2 = [share(k, 640, CUT) for k in (0, 1, 3)]
+    arrived(x1b)
+    s1.append(share(2, 0, 640))
+    s2.append(share(2, 640, CUT))
     arrived(ax)
-    arrived([s1])
+    arrived(s1)
 
     cols = []
     for h in range(2):
         acc = None
         for g in range(4):
-            w = w1[0, h, g].reshape(320, 640)
+            w = wb[0, h, g, :, :, 0:640].reshape(320, 640)
             part = jnp.dot(mx[g][:, 0:320], w, preferred_element_type=F32)
             acc = part if acc is None else acc + part
         cols.append(acc)
@@ -399,9 +439,10 @@
         return n2.at[j]
 
     gy = spread_y(block)
-    arrived([f2])
-    s2 = start(w2.at[c], w2.at[c], sib)
-    arrived([s2])
+    arrived(w2r)
+    done3 = wb.at[c, :, :, :, :, CUT:1280]
+    s2.append(start(done3, done3, sib))
+    arrived(s2)
 
     def feed(blocks, ship):
         m = ROWS * len(blocks)
@@ -410,8 +451,9 @@
 
             def hidden(i, carry):
                 at = pl.ds(pl.multiple_of(i * 128, 128), 128)
-                g = w2[0, h, :, :, :, at].reshape(D, 128)
-                v = w1[1, h, :, :, :, at].reshape(D, 128)
+                late = pl.ds(pl.multiple_of(640 + i * 128, 128), 128)
+                g = wb[0, h, :, :, :, late].reshape(D, 128)
+                v = wb[1, h, :, :, :, at].reshape(D, 128)
                 both = jnp.dot(
                     tokens, jnp.concatenate([g, v], axis=1), preferred_element_type=F32
                 )
@@ -425,7 +467,7 @@
         for n in range(5):
             acc = None
             for h in range(2):
-                w = w2[1, h].reshape(D, 640)[n * 256 : n * 256 + 256]
+                w = wb[1, h, :, :, :, 640:1280].reshape(D, 640)[n * 256 : n * 256 + 256]
                 part = lax.dot_general(hid[h, 0:m], w, NT, preferred_element_type=F32)
                 acc = part if acc is None else acc + part
             at = pl.ds(n * 256, 256)
@@ -464,7 +506,8 @@
 
     term = total(l1, x * 4 + y, plane, term)
     term = total(l2, z * 2 + c, column, term)
-    loss[...] = term
+    loss[0, 0] = jnp.max(term)
+    assert count[0] <= N_COPIES
 
     for d in sends:
         d.wait_send()
@@ -480,7 +523,8 @@
             d.wait_send()
 
 
-N_COPIES = 144
+N_COPIES = 160
+CUT = 1024
 
 
 def shards(
@@ -492,10 +536,10 @@
         kernel,
         out_shape=(
             jax.ShapeDtypeStruct((1, ROWS, D), F32),
-            jax.ShapeDtypeStruct((8, 128), F32),
+            jax.ShapeDtypeStruct((1, 1), F32),
         ),
         in_specs=[pl.BlockSpec(memory_space=pltpu.SMEM)] + [vm] * 11,
-        out_specs=(vm, vm),
+        out_specs=(vm, pl.BlockSpec(memory_space=pltpu.SMEM)),
         scratch_shapes=[
             pltpu.VMEM((40, 1536), BF),
             pltpu.VMEM((40, 1536), BF),
@@ -503,8 +547,7 @@
             pltpu.VMEM((2, 80, 128), BF),
             pltpu.VMEM((4, 80, 256), BF),
             pltpu.VMEM((2, 2, 4, 4, 80, 256), BF),
-            pltpu.VMEM((2, 2, 4, 4, 80, 640), BF),
-            pltpu.VMEM((2, 2, 4, 4, 80, 640), BF),
+            pltpu.VMEM((2, 2, 4, 4, 80, 1280), BF),
             pltpu.VMEM((8, ROWS, D), BF),
             pltpu.VMEM((5, L, 64), BF),
             pltpu.VMEM((5, L, 64), BF),
@@ -528,9 +571,9 @@
         ),
     )(
         tsteps, clean[0], noise[0], alpha_tab[None], weight_tab[None], norm1_gain[None],
-        norm2_gain[None], wqkv, wout, wgate, wvalue, wdown,
+        norm2_gain[None], wqkv, wout, wgate, wvalue, wdown.T,
     )
-    return den, loss[0, 0]
+    return den, loss.reshape(())
 
 
 def solution(mesh):

time: 154 us -> 140 us (0.909)
  Pallas kernels: 146 us -> 134 us
  local copies, waits for them, and re-layouts: 6.05 us -> 3.26 us
  between operations: 1.32 us -> 3.07 us
    pallas_call x1, Pallas kernels: 146 us -> 134 us  [shards(): pl.pallas_call(kernel, out_shape=(jax.ShapeDtypeStruct((1, ROWS, D), F32)...]
    unnamed x6 -> x5, local copies, waits for them, and re-layouts: 3.66 us -> 2.06 us
where the time goes in v3:
time: 140 us
  Pallas kernels  134 us (96%)
  local copies, waits for them, and re-layouts  3.26 us (2%)
  between operations  3.07 us (2%)
    pallas_call x1, Pallas kernels, shards(): pl.pallas_call(kernel, out_shape=(jax.ShapeDtypeStruct((1, ROWS, D), F32)...  134 us

profile of v3, /device:TPU:1, one launch (start us, length us, event | category | flops | bytes accessed | tf_op | source)
XLA Modules:
  0.0 139.9 jit_solution(8391165954123670192)
XLA Ops:
  0.6 0.0 copy-start
  1.3 0.0 copy-start.1
  1.3 0.0 copy-done
  1.3 0.6 broadcast_in_dim.14.gain1
  1.9 0.1 copy-done.1
  2.0 0.6 broadcast_in_dim.15.gain2
  2.6 133.6 %shard_map.131 = (f32[1,128,1280]{2,1,0:T(8,128)}, f32[1,1]{1,0:T(1,128)}) custom-call(s32[1]{0:T(128)S(6)} %copy.16.tsteps, bf16[128,1280]{1,0:T(8,128)(2,1)} %bitcast.6, bf16[128,1280]{1,0:T(8,128)(2,1)} %bitcast.7, f32[1,1000]{1,0:T(1,128)} %bitcast.9, f32[1,1000]{1,0:T(1,128)} %bitcast.10, f32[1,1280]{1,0:T(1,128)} %broadcast_in_dim.14.gain1, ...), custom_call_target="tpu_custom_call" | custom-call | tf_op jit(solution)/shard_map/pallas_call | solution.py:535
  136.2 2.0 %copy.17 = f32[1,128,1280]{2,1,0:T(8,128)} copy(f32[1,128,1280]{2,1,0:T(8,128)} %get-tuple-element.8) | data formatting | bytes 1310720
Async XLA Ops:
  0.6 0.7 copy-start
  1.3 0.7 copy-start.1

commit v4 on v3

--- a/solution.py
+++ b/solution.py
@@ -116,7 +116,7 @@
 
     noised[...] = (alpha * clean[...].astype(F32) + sigma * noise[...].astype(F32)).astype(BF)
     me = zh * 4 + y
-    n1[me] = normed(noised[...], gain1[...])
+    n1[me] = normed(noised[...], gain1[...].reshape(1, D))
 
     pl.semaphore_wait(barrier, len(greet))
     s0 = start(give, recv, sib)
@@ -224,40 +224,52 @@
             d.start()
         return ds
 
-    def even_ref(a, b, part):
+    def q_ref(a, b, part):
         rows = slice(None) if part is None else slice(48 * part, 48 + 32 * part)
-        return qw.at[c, a, b, x, rows, 0:128]
-
-    def odd_ref(a, b, part):
-        which = slice(None) if part is None else slice(2 * part, 2 * part + 2)
-        return qw.at[c, a, b, which, :, 128:256]
-
-    def w1_ref(a, b, part):
-        cols = slice(0, CUT) if part is None else slice(CUT // 2 * part, CUT // 2 * (part + 1))
+        return qw.at[c, a, b, x, rows]
+
+    def wa_ref(a, b, part):
+        cols = slice(0, 640) if part is None else slice(384 * part, 384 + 256 * part)
+        return wb.at[c, a, b, x, :, cols]
+
+    def wc_ref(a, b, part):
+        cols = slice(640, CUT) if part is None else slice(640 + 128 * part, 768 + 128 * part)
         return wb.at[c, a, b, x, :, cols]
 
     def w2_ref(a, b, part):
         which = slice(None) if part is None else slice(2 * part, 2 * part + 2)
         return wb.at[c, a, b, which, :, CUT:1280]
 
-    x1 = {}
-
-    def spread1(*ks):
-        for k in ks:
-            r = w1_ref(*slab2(k), None)
-            x1[k] = [start(r, r, d) for d in xs[:2]]
-
-    x1b = []
-
-    def relay1(*ks):
-        for k in ks:
-            arrived(x1[k])
-            a, b = slab2(k)
-            turn = 1 + 2 * a
-            r = wb.at[c, a, b, lax.rem(x + 4 - turn, 4), :, 0:CUT]
-            x1b.append(start(r, r, {"x": lax.rem(x + turn, 4)}))
-
-    spread1(0)
+    def spreader(ref):
+        got = {}
+
+        def spread(*ks):
+            for k in ks:
+                r = ref(*slab2(k), None)
+                got[k] = [start(r, r, d) for d in xs[:2]]
+
+        return got, spread
+
+    def relayer(got, lo, hi):
+        sent = []
+
+        def relay(*ks):
+            for k in ks:
+                arrived(got[k])
+                a, b = slab2(k)
+                turn = 1 + 2 * a
+                r = wb.at[c, a, b, lax.rem(x + 4 - turn, 4), :, lo:hi]
+                sent.append(start(r, r, {"x": lax.rem(x + turn, 4)}))
+
+        return sent, relay
+
+    xa, spreada = spreader(wa_ref)
+    xc, spreadc = spreader(wc_ref)
+    xa2, relaya = relayer(xa, 0, 640)
+    xc2, relayc = relayer(xc, 640, CUT)
+
+    ar = ring(wa_ref, 1)
+    spreada(0)
 
     homes = (jnp.logical_and(zh == 0, y == 0), jnp.logical_and(zh == 1, y == 3))
     alone = jnp.logical_or(*homes)
@@ -278,57 +290,90 @@
         def _():
             local.wait()
 
-    er = ring(even_ref, 1)
+    xq = []
+
+    def spreadq(*ks):
+        for k in ks:
+            r = q_ref(*slab2(k), None)
+            xq.extend([start(r, r, d) for d in xs[:2]])
+
+    def shareq(k):
+        r = qw.at[c, :, :, lax.rem(x + k, 4)]
+        return make(r, r, sib)
+
+    def share(k, lo, hi):
+        r = wb.at[c, :, :, lax.rem(x + k, 4), :, lo:hi]
+        return make(r, r, sib)
+
+    s2 = []
+
+    def share2(*ks):
+        for k in ks:
+            r = w2_ref(*slab2(k), None)
+            s2.append(start(r, r, sib))
+
+    def spread_far(low):
+        r = far(y).at[pl.ds(low, 64)]
+        return [start(r, r, d) for d in ys[:2]]
+
+    er = ring(q_ref, 1)
+    spreadq(0)
     cross(1)
-    odd = qw.at[c, zh, zl, x, :, 128:256]
-    ox = [start(odd, odd, d) for d in xs]
-
     arrived(er)
-    er = ring(even_ref, 2)
-    w1r = ring(w1_ref, 1)
-    arrived(ox)
-    dr = ring(odd_ref, 1)
-    arrived(er)
-    er = ring(even_ref, 3)
+    er = ring(q_ref, 2)
+    spreadq(-1, 1)
     cross(2)
-    arrived(dr)
-    dr = ring(odd_ref, 2)
-    arrived(er)
-    er = ring(even_ref, 4)
-    cross(3)
-    arrived(w1r)
-    spread1(-1, 1)
+    arrived(ar)
+    ar = ring(wa_ref, 2)
+    spreada(-1, 1)
     arrived(ty)
     ty = relay_y(near)
     arrived(er)
-    ex = [
-        start(qw.at[c, :, :, x, :, 0:128], qw.at[c, :, :, x, :, 0:128], d) for d in xs
-    ]
-    arrived(dr)
-    dr = ring(odd_ref, 3)
-    w1r = ring(w1_ref, 2)
-    relay1(0)
-    arrived(tz)
-    tf = spread_y(far)
-    arrived(dr)
-    dr = ring(odd_ref, 4)
-    arrived(w1r)
-    w1r = ring(w1_ref, 3)
-    spread1(-2, 2)
-    arrived(ex)
-    half = qw.at[c, :, :, :, :, 0:128]
-    sq = [start(half, half, sib)]
-    arrived(dr)
-    half = qw.at[c, :, :, :, :, 128:256]
-    sq.append(start(half, half, sib))
-    relay1(-1, 1)
+    er = ring(q_ref, 3)
+    spreadq(-2, 2)
+    cross(3)
+    arrived(tz[0:2])
+    tf = spread_far(0)
+    arrived(er)
+    er = ring(q_ref, 4)
+    spreadq(-3, 3)
+    arrived(ar)
+    ar = ring(wa_ref, 3)
+    arrived(er)
+    spreadq(4)
+    spreada(-2, 2)
+    arrived(tz[2:4])
+    tg = spread_far(64)
+    arrived(tf)
+    r = far(lax.rem(y + 3, 4)).at[pl.ds(0, 64)]
+    tr = [start(r, r, ys[0])]
     arrived(x2)
     w2r = ring(w2_ref, 1)
-    arrived(tf)
-    tf = relay_y(far)
-    arrived(w1r)
-    w1r = ring(w1_ref, 4)
-    spread1(-3, 3)
+    share2(0)
+    arrived(xq)
+    rq = []
+    for a in range(2):
+        turn = 1 + 2 * a
+        r = qw.at[c, a, :, lax.rem(x + 4 - turn, 4)]
+        rq.append(start(r, r, {"x": lax.rem(x + turn, 4)}))
+    sq = [shareq(k) for k in (0, 1, 3)]
+    for d in sq:
+        d.start()
+    relaya(0)
+    arrived(ar)
+    ar = ring(wa_ref, 4)
+    spreada(-3, 3)
+    relaya(-1, 1)
+    arrived(tg)
+    r = far(lax.rem(y + 1, 4)).at[pl.ds(64, 64)]
+    tr.append(start(r, r, ys[1]))
+    cr = ring(wc_ref, 1)
+    arrived(rq)
+    sq.append(shareq(2))
+    sq[3].start()
+    arrived(w2r)
+    w2r = ring(w2_ref, 2)
+    share2(-1, 1)
     arrived(ty)
     arrived(sq)
 
@@ -361,66 +406,57 @@
         put(vh, 2, halves[2])
 
     project(zh)
-    relay1(-2, 2)
-    arrived(tf)
+    arrived(ar)
+    spreada(4)
+    relaya(-2, 2)
+    arrived(cr)
+    cr = ring(wc_ref, 2)
+    spreadc(0)
+    arrived(tr)
     project(1 - zh)
-    arrived(w1r)
-    spread1(4)
-    arrived(w2r)
-    w2r = ring(w2_ref, 2)
-
-    held = w2r
-    w2r = [hop(w2_ref, 3, True), hop(w2_ref, 3, False)]
-    abase = count[0]
-    count[0] += 3
-
-    def give_tile(t, i):
-        return pltpu.make_async_remote_copy(
-            src_ref=mo.at[i], dst_ref=mx.at[y], send_sem=ss.at[abase + t],
-            recv_sem=rs.at[abase + t], device_id={"y": i}, device_id_type=MESH,
-        )
-
-    def attend(t, carry):
-        i = lax.rem(y + t + 1, 4)
+
+    ax = []
+
+    def attend(k):
+        i = lax.rem(y + k, 4)
         r = pl.ds(pl.multiple_of(zh * 512 + i * 128, 128), 128)
-
-        @pl.when(t == 2)
-        def _():
-            arrived(held)
-            for d in w2r:
-                d.start()
-
         for n in range(5):
             s = lax.dot_general(qh[n, r], kh[n], NT, preferred_element_type=F32)
             p = jnp.exp(s - jnp.max(s, axis=1, keepdims=True))
             total = jnp.sum(p, axis=1, keepdims=True)
             o = jnp.dot(p.astype(BF), vh[n], preferred_element_type=F32) / total
             mo[i, :, n * 64 : n * 64 + 64] = o.astype(BF)
-
-        @pl.when(t < 3)
-        def _():
-            give_tile(t, i).start()
-
-        return carry
-
-    lax.fori_loop(0, 4, attend, 0)
-    ax = [give_tile(t, lax.rem(y + t + 1, 4)) for t in range(3)]
-    sends.extend(ax)
-
-    mx[y] = mo[y]
+        if k:
+            ax.append(start(mo.at[i], mx.at[y], {"y": i}))
+
+    attend(2)
+    relaya(-3, 3)
+    spreadc(-1, 1)
+    arrived(w2r)
+    w2r = ring(w2_ref, 3)
+    share2(-2, 2)
+    attend(1)
+    arrived(cr)
+    cr = ring(wc_ref, 3)
+    relaya(4)
+    spreadc(-2, 2)
+    s1 = [share(k, 0, 640) for k in (0, 1, 3)]
+    for d in s1:
+        d.start()
+    attend(3)
     arrived(w2r)
     w2r = ring(w2_ref, 4)
-    relay1(-3, 3, 4)
-
-    def share(k, lo, hi):
-        r = wb.at[c, :, :, lax.rem(x + k, 4), :, lo:hi]
-        return start(r, r, sib)
-
-    s1 = [share(k, 0, 640) for k in (0, 1, 3)]
-    s2 = [share(k, 640, CUT) for k in (0, 1, 3)]
-    arrived(x1b)
+    share2(-3, 3)
+    relayc(0, -1, 1)
+    attend(0)
+    mx[y] = mo[y]
+    arrived(cr)
+    cr = ring(wc_ref, 4)
+    spreadc(-3, 3)
+    arrived(xa2)
     s1.append(share(2, 0, 640))
-    s2.append(share(2, 640, CUT))
+    s1[3].start()
+    relayc(-2, 2)
     arrived(ax)
     arrived(s1)
 
@@ -433,20 +469,33 @@
             acc = part if acc is None else acc + part
         cols.append(acc)
     resid[...] = (noised[...].astype(F32) + jnp.concatenate(cols, axis=1)).astype(BF)
-    n2[y] = normed(resid[...], gain2[...])
-
-    def block(j):
-        return n2.at[j]
-
-    gy = spread_y(block)
+    n2[y] = normed(resid[...], gain2[...].reshape(1, D))
+
+    gy = [start(n2.at[y], n2.at[y], d) for d in ys[:2]]
+    arrived(cr)
+    spreadc(4)
+    relayc(-3, 3)
     arrived(w2r)
-    done3 = wb.at[c, :, :, :, :, CUT:1280]
-    s2.append(start(done3, done3, sib))
+    share2(4)
+    relayc(4)
+    s1b = [share(k, 640, CUT) for k in (0, 1, 3)]
+    for d in s1b:
+        d.start()
+    arrived(gy)
+    up, down = lax.rem(y + 1, 4), lax.rem(y + 3, 4)
+    gr = []
+    for j, low, d in ((down, 0, ys[0]), (up, 64, ys[1])):
+        r = n2.at[j, pl.ds(low, 64)]
+        gr.append(start(r, r, d))
+    arrived(xc2)
+    s1b.append(share(2, 640, CUT))
+    s1b[3].start()
     arrived(s2)
+    arrived(s1b)
 
     def feed(blocks, ship):
-        m = ROWS * len(blocks)
-        tokens = jnp.concatenate([n2[j] for j in blocks], axis=0) if m > ROWS else n2[blocks[0]]
+        m = sum(n for j, r, n in blocks)
+        tokens = jnp.concatenate([n2[j, r : r + n] for j, r, n in blocks], axis=0)
         for h in range(2):
 
             def hidden(i, carry):
@@ -471,21 +520,22 @@
                 part = lax.dot_general(hid[h, 0:m], w, NT, preferred_element_type=F32)
                 acc = part if acc is None else acc + part
             at = pl.ds(n * 256, 256)
-            for q, j in enumerate(blocks):
-                part = acc[q * ROWS : q * ROWS + ROWS].astype(BF)
+            q = 0
+            for j, r, k in blocks:
+                part = acc[q : q + k].astype(BF)
+                q += k
+                rows = pl.ds(r, k)
                 if ship:
-                    fs[j, :, at] = part
-                    copies.append(start(fs.at[j, :, at], ffin.at[y, :, at], {"y": j}))
+                    fs[j, rows, at] = part
+                    copies.append(start(fs.at[j, rows, at], ffin.at[y, rows, at], {"y": j}))
                 else:
-                    ffin[j, :, at] = part
+                    ffin[j, rows, at] = part
         return copies
 
-    feed([y], False)
-    arrived(gy)
-    gy = relay_y(block)
-    ry = feed([lax.rem(y + 1, 4), lax.rem(y + 3, 4)], True)
-    arrived(gy)
-    ry += feed([lax.rem(y + 2, 4)], True)
+    ry = feed([(up, 0, ROWS), (down, 0, ROWS)], True)
+    arrived(gr)
+    ry += feed([(lax.rem(y + 2, 4), 0, ROWS)], True)
+    feed([(y, 0, ROWS)], False)
     arrived(ry)
     prediction = resid[...].astype(F32)
     for j in range(4):
@@ -523,8 +573,8 @@
             d.wait_send()
 
 
-N_COPIES = 160
-CUT = 1024
+N_COPIES = 208
+CUT = 896
 
 
 def shards(
@@ -570,8 +620,8 @@
             collective_id=0, has_side_effects=True, vmem_limit_bytes=60 * 2**20
         ),
     )(
-        tsteps, clean[0], noise[0], alpha_tab[None], weight_tab[None], norm1_gain[None],
-        norm2_gain[None], wqkv, wout, wgate, wvalue, wdown.T,
+        tsteps, clean[0], noise[0], alpha_tab[None], weight_tab[None], norm1_gain,
+        norm2_gain, wqkv, wout, wgate, wvalue, wdown.T,
     )
     return den, loss.reshape(())
 

time: 140 us -> 126 us (0.900)
  Pallas kernels: 134 us -> 121 us
    pallas_call x1, Pallas kernels: 134 us -> 121 us  [shards(): pl.pallas_call(kernel, out_shape=(jax.ShapeDtypeStruct((1, ROWS, D), F32)...]
where the time goes in v4:
time: 126 us
  Pallas kernels  121 us (96%)
  between operations  3.04 us (2%)
  local copies, waits for them, and re-layouts  1.97 us (2%)
    pallas_call x1, Pallas kernels, shards(): pl.pallas_call(kernel, out_shape=(jax.ShapeDtypeStruct((1, ROWS, D), F32)...  121 us

profile of v4, /device:TPU:1, one launch (start us, length us, event | category | flops | bytes accessed | tf_op | source)
XLA Modules:
  0.0 126.1 jit_solution(2568702091390913187)
XLA Ops:
  1.3 121.1 %shard_map.131 = (f32[1,128,1280]{2,1,0:T(8,128)}, f32[1,1]{1,0:T(1,128)}) custom-call(s32[1]{0:T(128)S(6)} %copy.16.tsteps, bf16[128,1280]{1,0:T(8,128)(2,1)} %bitcast.6, bf16[128,1280]{1,0:T(8,128)(2,1)} %bitcast.7, f32[1,1000]{1,0:T(1,128)} %bitcast.9, f32[1,1000]{1,0:T(1,128)} %bitcast.10, f32[1280]{0:T(1024)} %gain1.1, f32[1280]{0:T(1024)} %gain2.1, ...), custom_call_target="tpu_custom_call" | custom-call | tf_op jit(solution)/shard_map/pallas_call | solution.py:585
  122.4 2.0 %copy.17 = f32[1,128,1280]{2,1,0:T(8,128)} copy(f32[1,128,1280]{2,1,0:T(8,128)} %get-tuple-element.8) | data formatting | bytes 1310720

commit v5 on v4

--- a/solution.py
+++ b/solution.py
@@ -120,6 +120,14 @@
 
     pl.semaphore_wait(barrier, len(greet))
     s0 = start(give, recv, sib)
+    tz = []
+
+    def cross(*ks):
+        for k in ks:
+            r = n1.at[me, pl.ds(32 * k, 32)]
+            tz.append(start(r, r, {"zh": 1 - zh}))
+
+    cross(0)
 
     def spread_y(ref):
         return [start(ref(y), ref(y), d) for d in ys[:2]]
@@ -194,25 +202,6 @@
         t = lax.rem(z + k + 8, 8)
         return t // 4, lax.rem(t, 4)
 
-    own2 = wb.at[c, zh, zl, x, :, CUT:1280]
-    x2 = [start(own2, own2, d) for d in xs]
-    ty = spread_y(near)
-    tz = []
-
-    def cross(*ks):
-        for k in ks:
-            r = n1.at[me, pl.ds(32 * k, 32)]
-            tz.append(start(r, r, {"zh": 1 - zh}))
-
-    cross(0)
-
-    @pl.when(c == 0)
-    def _():
-        for d in wy:
-            d.wait_recv()
-        parts = [wt[j][:, 0:160].astype(F32) for j in range(4)]
-        wb[0, zh, zl, x, :, 0:640] = jnp.concatenate(parts, axis=1).astype(BF)
-
     def hop(ref, k, forward):
         a, b = slab2(-(k - 1) if forward else k - 1)
         r = ref(a, b, None if k < 4 else 1 - int(forward))
@@ -267,6 +256,18 @@
     xc, spreadc = spreader(wc_ref)
     xa2, relaya = relayer(xa, 0, 640)
     xc2, relayc = relayer(xc, 640, CUT)
+
+    own2 = wb.at[c, zh, zl, x, :, CUT:1280]
+    x2 = [start(own2, own2, d) for d in xs]
+    cr = ring(wc_ref, 1)
+    spreadc(0)
+    ty = spread_y(near)
+    @pl.when(c == 0)
+    def _():
+        for d in wy:
+            d.wait_recv()
+        parts = [wt[j][:, 0:160].astype(F32) for j in range(4)]
+        wb[0, zh, zl, x, :, 0:640] = jnp.concatenate(parts, axis=1).astype(BF)
 
     ar = ring(wa_ref, 1)
     spreada(0)
@@ -290,12 +291,16 @@
         def _():
             local.wait()
 
-    xq = []
-
-    def spreadq(*ks):
+    xq, spreadq = spreader(q_ref)
+    rq = []
+
+    def relayq(*ks):
         for k in ks:
-            r = q_ref(*slab2(k), None)
-            xq.extend([start(r, r, d) for d in xs[:2]])
+            arrived(xq[k])
+            a, b = slab2(k)
+            turn = 1 + 2 * a
+            r = qw.at[c, a, b, lax.rem(x + 4 - turn, 4)]
+            rq.append(start(r, r, {"x": lax.rem(x + turn, 4)}))
 
     def shareq(k):
         r = qw.at[c, :, :, lax.rem(x + k, 4)]
@@ -331,46 +336,46 @@
     arrived(er)
     er = ring(q_ref, 3)
     spreadq(-2, 2)
+    relayq(0)
     cross(3)
     arrived(tz[0:2])
     tf = spread_far(0)
+    arrived(ar)
+    ar = ring(wa_ref, 3)
+    spreada(-2, 2)
     arrived(er)
     er = ring(q_ref, 4)
     spreadq(-3, 3)
-    arrived(ar)
-    ar = ring(wa_ref, 3)
+    relayq(-1, 1)
     arrived(er)
     spreadq(4)
-    spreada(-2, 2)
+    relayq(-2, 2)
     arrived(tz[2:4])
     tg = spread_far(64)
+    arrived(ar)
+    ar = ring(wa_ref, 4)
     arrived(tf)
     r = far(lax.rem(y + 3, 4)).at[pl.ds(0, 64)]
     tr = [start(r, r, ys[0])]
     arrived(x2)
     w2r = ring(w2_ref, 1)
     share2(0)
-    arrived(xq)
-    rq = []
-    for a in range(2):
-        turn = 1 + 2 * a
-        r = qw.at[c, a, :, lax.rem(x + 4 - turn, 4)]
-        rq.append(start(r, r, {"x": lax.rem(x + turn, 4)}))
+    relayq(-3, 3, 4)
     sq = [shareq(k) for k in (0, 1, 3)]
     for d in sq:
         d.start()
-    relaya(0)
-    arrived(ar)
-    ar = ring(wa_ref, 4)
     spreada(-3, 3)
-    relaya(-1, 1)
+    relaya(0, -1, 1)
     arrived(tg)
     r = far(lax.rem(y + 1, 4)).at[pl.ds(64, 64)]
     tr.append(start(r, r, ys[1]))
-    cr = ring(wc_ref, 1)
     arrived(rq)
     sq.append(shareq(2))
     sq[3].start()
+    arrived(ar)
+    spreada(4)
+    arrived(cr)
+    cr = ring(wc_ref, 2)
     arrived(w2r)
     w2r = ring(w2_ref, 2)
     share2(-1, 1)
@@ -406,12 +411,8 @@
         put(vh, 2, halves[2])
 
     project(zh)
-    arrived(ar)
-    spreada(4)
     relaya(-2, 2)
-    arrived(cr)
-    cr = ring(wc_ref, 2)
-    spreadc(0)
+    spreadc(-1, 1)
     arrived(tr)
     project(1 - zh)
 
@@ -431,7 +432,6 @@
 
     attend(2)
     relaya(-3, 3)
-    spreadc(-1, 1)
     arrived(w2r)
     w2r = ring(w2_ref, 3)
     share2(-2, 2)
@@ -444,12 +444,12 @@
     for d in s1:
         d.start()
     attend(3)
+    relayc(0, -1, 1)
+    attend(0)
+    mx[y] = mo[y]
     arrived(w2r)
     w2r = ring(w2_ref, 4)
     share2(-3, 3)
-    relayc(0, -1, 1)
-    attend(0)
-    mx[y] = mo[y]
     arrived(cr)
     cr = ring(wc_ref, 4)
     spreadc(-3, 3)
@@ -481,12 +481,6 @@
     s1b = [share(k, 640, CUT) for k in (0, 1, 3)]
     for d in s1b:
         d.start()
-    arrived(gy)
-    up, down = lax.rem(y + 1, 4), lax.rem(y + 3, 4)
-    gr = []
-    for j, low, d in ((down, 0, ys[0]), (up, 64, ys[1])):
-        r = n2.at[j, pl.ds(low, 64)]
-        gr.append(start(r, r, d))
     arrived(xc2)
     s1b.append(share(2, 640, CUT))
     s1b[3].start()
@@ -511,7 +505,7 @@
                 hid[h, 0:m, at] = act.astype(BF)
                 return carry
 
-            lax.fori_loop(0, 5, hidden, 0)
+            lax.fori_loop(0, 5, hidden, 0, unroll=True)
         copies = []
         for n in range(5):
             acc = None
@@ -532,10 +526,16 @@
                     ffin[j, rows, at] = part
         return copies
 
+    feed([(y, 0, ROWS)], False)
+    arrived(gy)
+    up, down = lax.rem(y + 1, 4), lax.rem(y + 3, 4)
+    gr = []
+    for j, low, d in ((down, 0, ys[0]), (up, 64, ys[1])):
+        r = n2.at[j, pl.ds(low, 64)]
+        gr.append(start(r, r, d))
     ry = feed([(up, 0, ROWS), (down, 0, ROWS)], True)
     arrived(gr)
     ry += feed([(lax.rem(y + 2, 4), 0, ROWS)], True)
-    feed([(y, 0, ROWS)], False)
     arrived(ry)
     prediction = resid[...].astype(F32)
     for j in range(4):
@@ -573,7 +573,7 @@
             d.wait_send()
 
 
-N_COPIES = 208
+N_COPIES = 224
 CUT = 896
 
 

time: 126 us -> 122 us (0.968)
  Pallas kernels: 121 us -> 117 us
    pallas_call x1, Pallas kernels: 121 us -> 117 us  [shards(): pl.pallas_call(kernel, out_shape=(jax.ShapeDtypeStruct((1, ROWS, D), F32)...]
where the time goes in v5:
time: 122 us
  Pallas kernels  117 us (96%)
  between operations  3.04 us (2%)
  local copies, waits for them, and re-layouts  1.97 us (2%)
    pallas_call x1, Pallas kernels, shards(): pl.pallas_call(kernel, out_shape=(jax.ShapeDtypeStruct((1, ROWS, D), F32)...  117 us

profile of v5, /device:TPU:1, one launch (start us, length us, event | category | flops | bytes accessed | tf_op | source)
XLA Modules:
  0.0 121.9 jit_solution(1933955123196672097)
XLA Ops:
  1.3 116.9 %shard_map.131 = (f32[1,128,1280]{2,1,0:T(8,128)}, f32[1,1]{1,0:T(1,128)}) custom-call(s32[1]{0:T(128)S(6)} %copy.16.tsteps, bf16[128,1280]{1,0:T(8,128)(2,1)} %bitcast.6, bf16[128,1280]{1,0:T(8,128)(2,1)} %bitcast.7, f32[1,1000]{1,0:T(1,128)} %bitcast.9, f32[1,1000]{1,0:T(1,128)} %bitcast.10, f32[1280]{0:T(1024)} %gain1.1, f32[1280]{0:T(1024)} %gain2.1, ...), custom_call_target="tpu_custom_call" | custom-call | tf_op jit(solution)/shard_map/pallas_call | solution.py:585
  118.2 2.0 %copy.17 = f32[1,128,1280]{2,1,0:T(8,128)} copy(f32[1,128,1280]{2,1,0:T(8,128)} %get-tuple-element.8) | data formatting | bytes 1310720

commit v6 on v5

--- a/solution.py
+++ b/solution.py
@@ -444,19 +444,19 @@
     for d in s1:
         d.start()
     attend(3)
+    attend(0)
     relayc(0, -1, 1)
-    attend(0)
     mx[y] = mo[y]
     arrived(w2r)
     w2r = ring(w2_ref, 4)
-    share2(-3, 3)
     arrived(cr)
     cr = ring(wc_ref, 4)
-    spreadc(-3, 3)
     arrived(xa2)
     s1.append(share(2, 0, 640))
     s1[3].start()
+    spreadc(-3, 3)
     relayc(-2, 2)
+    share2(-3, 3)
     arrived(ax)
     arrived(s1)
 
@@ -526,7 +526,6 @@
                     ffin[j, rows, at] = part
         return copies
 
-    feed([(y, 0, ROWS)], False)
     arrived(gy)
     up, down = lax.rem(y + 1, 4), lax.rem(y + 3, 4)
     gr = []
@@ -536,12 +535,13 @@
     ry = feed([(up, 0, ROWS), (down, 0, ROWS)], True)
     arrived(gr)
     ry += feed([(lax.rem(y + 2, 4), 0, ROWS)], True)
+    feed([(y, 0, ROWS)], False)
     arrived(ry)
     prediction = resid[...].astype(F32)
     for j in range(4):
         prediction = prediction + ffin[j].astype(F32)
     denoised = (noised[...].astype(F32) - sigma * prediction) / alpha
-    den[0] = denoised
+    den[0] = denoised * 0.5
     error = denoised - clean[...].astype(F32)
     rowsum = jnp.sum(error * error, axis=1, keepdims=True)
     term = jnp.sum(rowsum, axis=0, keepdims=True) * weight
@@ -623,7 +623,7 @@
         tsteps, clean[0], noise[0], alpha_tab[None], weight_tab[None], norm1_gain,
         norm2_gain, wqkv, wout, wgate, wvalue, wdown.T,
     )
-    return den, loss.reshape(())
+    return den * 2.0, loss.reshape(())
 
 
 def solution(mesh):

time: 122 us -> 120 us (0.984)
  Pallas kernels: 117 us -> 115 us
  other arithmetic: 0 us -> 1.97 us
  local copies, waits for them, and re-layouts: 1.97 us -> 0 us
    mul x0 -> x1, other arithmetic: none -> 1.97 us  [shards(): return (den * 2.0, loss.reshape(()))]
    unnamed x1 -> x0, local copies, waits for them, and re-layouts: 1.97 us -> none
    pallas_call x1, Pallas kernels: 117 us -> 115 us  [shards(): pl.pallas_call(kernel, out_shape=(jax.ShapeDtypeStruct((1, ROWS, D), F32)...]
where the time goes in v6:
time: 120 us
  Pallas kernels  115 us (96%)
  between operations  3.04 us (3%)
  other arithmetic  1.97 us (2%)
    pallas_call x1, Pallas kernels, shards(): pl.pallas_call(kernel, out_shape=(jax.ShapeDtypeStruct((1, ROWS, D), F32)...  115 us

profile of v6, /device:TPU:1, one launch (start us, length us, event | category | flops | bytes accessed | tf_op | source)
XLA Modules:
  0.0 120.3 jit_solution(15146179924196707608)
XLA Ops:
  1.3 115.3 %shard_map.131 = (f32[1,128,1280]{2,1,0:T(8,128)}, f32[1,1]{1,0:T(1,128)}) custom-call(s32[1]{0:T(128)S(6)} %copy.15.tsteps, bf16[128,1280]{1,0:T(8,128)(2,1)} %bitcast.6, bf16[128,1280]{1,0:T(8,128)(2,1)} %bitcast.7, f32[1,1000]{1,0:T(1,128)} %bitcast.9, f32[1,1000]{1,0:T(1,128)} %bitcast.10, f32[1280]{0:T(1024)} %gain1.1, f32[1280]{0:T(1024)} %gain2.1, ...), custom_call_target="tpu_custom_call" | custom-call | tf_op jit(solution)/shard_map/pallas_call | solution.py:585
  116.5 2.0 %broadcast_multiply_fusion = f32[1,128,1280]{2,1,0:T(8,128)} fusion(f32[1,128,1280]{2,1,0:T(8,128)} %get-tuple-element.4), kind=kLoop, calls=%fused_computation | loop fusion | flops 163840 | bytes 1310720 | tf_op jit(solution)/shard_map/mul | solution.py:626

commit v7 on v6

--- a/solution.py
+++ b/solution.py
@@ -30,7 +30,7 @@
     tsteps, clean, noise, alpha_tab, weight_tab, gain1, gain2, wqkv, wout, wgate, wvalue, wdown,
     den, loss,
     keep, give, recv, qs, wt, qw, wb, n1, qh, kh, vh, mo, mx, n2, hid, fs, ffin, noised, resid,
-    l1, l2, ss, rs, ls,
+    l1, l2, dbuf, ss, rs, ls, ds,
 ):
     zl, x, c, zh, y = (lax.axis_index(a) for a in AXES)
     z = zh * 4 + zl
@@ -541,7 +541,9 @@
     for j in range(4):
         prediction = prediction + ffin[j].astype(F32)
     denoised = (noised[...].astype(F32) - sigma * prediction) / alpha
-    den[0] = denoised * 0.5
+    dbuf[0] = denoised * 0.5
+    out = pltpu.make_async_copy(dbuf, den, ds)
+    out.start()
     error = denoised - clean[...].astype(F32)
     rowsum = jnp.sum(error * error, axis=1, keepdims=True)
     term = jnp.sum(rowsum, axis=0, keepdims=True) * weight
@@ -557,6 +559,7 @@
     term = total(l1, x * 4 + y, plane, term)
     term = total(l2, z * 2 + c, column, term)
     loss[0, 0] = jnp.max(term)
+    out.wait()
     assert count[0] <= N_COPIES
 
     for d in sends:
@@ -589,7 +592,7 @@
             jax.ShapeDtypeStruct((1, 1), F32),
         ),
         in_specs=[pl.BlockSpec(memory_space=pltpu.SMEM)] + [vm] * 11,
-        out_specs=(vm, pl.BlockSpec(memory_space=pltpu.SMEM)),
+        out_specs=(pl.BlockSpec(memory_space=pl.ANY), pl.BlockSpec(memory_space=pltpu.SMEM)),
         scratch_shapes=[
             pltpu.VMEM((40, 1536), BF),
             pltpu.VMEM((40, 1536), BF),
@@ -612,8 +615,10 @@
             pltpu.VMEM((ROWS, D), BF),
             pltpu.VMEM((16, 8, 128), F32),
             pltpu.VMEM((16, 8, 128), F32),
+            pltpu.VMEM((1, ROWS, D), F32),
             pltpu.SemaphoreType.DMA((N_COPIES,)),
             pltpu.SemaphoreType.DMA((N_COPIES,)),
+            pltpu.SemaphoreType.DMA,
             pltpu.SemaphoreType.DMA,
         ],
         compiler_params=pltpu.CompilerParams(

time: 120 us -> 120 us (level)
  no operation moved by 1% of the time
where the time goes in v7:
time: 120 us
  Pallas kernels  115 us (96%)
  between operations  3.04 us (3%)
  other arithmetic  1.97 us (2%)
    pallas_call x1, Pallas kernels, shards(): pl.pallas_call(kernel, out_shape=(jax.ShapeDtypeStruct((1, ROWS, D), F32)...  115 us

profile of v7, /device:TPU:1, one launch (start us, length us, event | category | flops | bytes accessed | tf_op | source)
XLA Modules:
  0.0 119.9 jit_solution(16008376916487163692)
XLA Ops:
  1.3 114.9 %shard_map.131 = (f32[1,128,1280]{2,1,0:T(8,128)}, f32[1,1]{1,0:T(1,128)}) custom-call(s32[1]{0:T(128)S(6)} %copy.15.tsteps, bf16[128,1280]{1,0:T(8,128)(2,1)} %bitcast.6, bf16[128,1280]{1,0:T(8,128)(2,1)} %bitcast.7, f32[1,1000]{1,0:T(1,128)} %bitcast.9, f32[1,1000]{1,0:T(1,128)} %bitcast.10, f32[1280]{0:T(1024)} %gain1.1, f32[1280]{0:T(1024)} %gain2.1, ...), custom_call_target="tpu_custom_call" | custom-call | tf_op jit(solution)/shard_map/pallas_call | solution.py:588
  116.2 2.0 %broadcast_multiply_fusion = f32[1,128,1280]{2,1,0:T(8,128)} fusion(f32[1,128,1280]{2,1,0:T(8,128)} %get-tuple-element.4), kind=kLoop, calls=%fused_computation | loop fusion | flops 163840 | bytes 1310720 | tf_op jit(solution)/shard_map/mul | solution.py:631
